TPU v7x, 32 devices: a whole 2x2x4 slice. The times are simulated.
32 devices in a mesh: req: 8 (over z, x), mlp: 4 (over y, core).
Axes of the slice: x: 2, y: 2, z: 4, core: 2. Of those that a mesh axis runs over, the one named last changes fastest.
Arguments:
- tokens: bfloat16 [8192, 2048], P('req'), may hold values from -6 to 6
- first_gain: float32 [2048], replicated, may hold values from 0.5 to 1.5
- joined_weight: bfloat16 [2048, 6144], P(None, 'mlp'), may hold values from -0.125 to 0.125
- dense_weight: bfloat16 [2048, 2048], P('mlp'), may hold values from -0.125 to 0.125
- adapter_down: bfloat16 [64, 16, 2048], P('req', None, 'mlp'), may hold values from -0.125 to 0.125
- adapter_up: bfloat16 [64, 16, 2048], P('req'), may hold values from -1.5 to 1.5
- adapter_ids: int32 [64], replicated, may hold values from 0 to 63, as said below
- adapter_rows: int32 [64], replicated, may hold values from 0 to 63, each once
- second_gain: float32 [2048], replicated, may hold values from 0.5 to 1.5
- up_weight: bfloat16 [2048, 8192], P(None, 'mlp'), may hold values from -0.125 to 0.125
- down_weight: bfloat16 [8192, 2048], P('mlp'), may hold values from -0.0625 to 0.0625
- page_pool: bfloat16 [96, 128, 4096], P('req', None, 'mlp'), may hold values from -100 to 100
- page_table: int32 [16, 4], P('req'), may hold values from 0 to 11, as said below
- group_index: int32 [64], P('req'), may hold values from 0 to 1
- lengths: int32 [64], P('req'), may hold values from 1 to 128, as said below
- migrants: int32 [32], P('req'), may hold values from 0 to 7, as said below
- landing: int32 [32], replicated, may hold values from 0 to 63, as said below
Outputs:
- layer_out: bfloat16 [8192, 2048], P(('req', 'mlp'))
- page_out: bfloat16 [64, 128, 4096], P('req', None, 'mlp')
Inputs may be any that keep to these rules, and one draw needn't show every extreme that they name: `adapter_ids`: the requests name exactly 16 distinct adapters in all. `lengths`: each request owner holds at least one request of 128 tokens. `page_table`: the 8 entries of one owner's rows are distinct. `migrants`: entries m // 4 = o name 4 distinct requests of owner o. `landing`: A rearrangement of the slots (m // 4) * 8 + migrants[m] of all migrating requests; the 4 requests of one owner land on 4 distinct other owners, and every owner receives exactly 4 of them.
All inputs are finite; a program needn't handle non-finite values.
Results may differ from a plain program's by a relative error of at most 0.013.
The roundings to bfloat16 on the way count: a program that leaves them out, or rounds other values in their place, can miss the bound.
Values may be sent and summed in bfloat16 or wider, within the bound.
A program may use at most 192 MiB of HBM per device.

v0:
```python
import math

import jax
import jax.numpy as jnp
from jax import lax
from jax.sharding import PartitionSpec as P

HEADS = 16
HD = 128
ADAPTERS = 64


EPS = 1e-05


def layer_norm(values, gain):
    values = values.astype(jnp.float32)
    mean = jnp.mean(values, axis=-1, keepdims=True)
    centred = values - mean
    variance = jnp.mean(centred * centred, axis=-1, keepdims=True)
    return (centred * lax.rsqrt(variance + EPS) * gain).astype(jnp.bfloat16)


def gelu_tanh(value):
    return 0.5 * value * (1.0 + jnp.tanh(0.7978845608 * (value + 0.044715 * value * value * value)))


def attend(queries, keys, values, prefix_keys, prefix_values, lens, slopes):
    scale = 1.0 / math.sqrt(queries.shape[-1])
    own_len = queries.shape[1]
    pre_len = prefix_keys.shape[1]
    s_pre = (
        jnp.einsum("rihe,rphe->rhip", queries, prefix_keys, preferred_element_type=jnp.float32)
        * scale
    )
    s_own = jnp.einsum("rihe,rjhe->rhij", queries, keys, preferred_element_type=jnp.float32) * scale
    own_pos = jnp.arange(own_len).astype(jnp.float32)
    pre_pos = jnp.arange(pre_len).astype(jnp.float32)
    s_pre = (
        s_pre
        - slopes[None, :, None, None]
        * ((pre_len + own_pos)[:, None] - pre_pos[None, :])[None, None]
    )
    s_own = s_own - slopes[None, :, None, None] * (own_pos[:, None] - own_pos[None, :])[None, None]
    steps = jnp.arange(own_len, dtype=jnp.int32)
    allowed = (steps[None, :] <= steps[:, None])[None, None] & (
        steps[None, None, None, :] < lens[:, None, None, None]
    )
    s_own = jnp.where(allowed, s_own, -jnp.inf)
    top = jnp.maximum(jnp.max(s_pre, axis=-1), jnp.max(s_own, axis=-1))[..., None]
    e_pre = jnp.exp(s_pre - top)
    e_own = jnp.exp(s_own - top)
    total = jnp.sum(e_pre, axis=-1, keepdims=True) + jnp.sum(e_own, axis=-1, keepdims=True)
    w_pre = (e_pre / total).astype(jnp.bfloat16)
    w_own = (e_own / total).astype(jnp.bfloat16)
    mixed = jnp.einsum("rhip,rphe->rihe", w_pre, prefix_values, preferred_element_type=jnp.float32)
    mixed = mixed + jnp.einsum("rhij,rjhe->rihe", w_own, values, preferred_element_type=jnp.float32)
    return mixed.astype(jnp.bfloat16)


def shards(
    tokens,
    first_gain,
    joined_weight,
    dense_weight,
    adapter_down,
    adapter_up,
    adapter_ids,
    adapter_rows,
    second_gain,
    up_weight,
    down_weight,
    page_pool,
    page_table,
    group_index,
    lengths,
    migrants,
    landing,
):
    mlp_count = lax.axis_size("mlp")
    req_index = lax.axis_index("req")
    mlp_index = lax.axis_index("mlp")
    requests = lengths.shape[0]
    slot = tokens.shape[0] // requests
    local_heads = joined_weight.shape[1] // (3 * HD)
    row_share = tokens.shape[0] // mlp_count
    own_requests = requests // mlp_count
    normed = layer_norm(tokens, first_gain)
    joined = jnp.dot(normed, joined_weight, preferred_element_type=jnp.float32).astype(jnp.bfloat16)
    joined = joined.reshape(requests, slot, local_heads, 3, HD)
    valid = jnp.arange(slot, dtype=jnp.int32)[None, :] < lengths[:, None]
    fresh = joined[:, :, :, 1:, :].reshape(requests, slot, local_heads * 2 * HD)
    fresh = jnp.where(valid[:, :, None], fresh, jnp.zeros((), jnp.bfloat16))
    pages = page_table[group_index]
    pool_view = page_pool.reshape(page_pool.shape[0], page_pool.shape[1], local_heads, 2, HD)
    prefix = pool_view[pages].reshape(
        requests, pages.shape[1] * page_pool.shape[1], local_heads, 2, HD
    )
    head_pos = (mlp_index * local_heads + jnp.arange(local_heads, dtype=jnp.int32)).astype(
        jnp.float32
    )
    slopes = jnp.exp2(-8.0 * (head_pos + 1.0) / HEADS)
    attended = attend(
        joined[:, :, :, 0],
        joined[:, :, :, 1],
        joined[:, :, :, 2],
        prefix[:, :, :, 0],
        prefix[:, :, :, 1],
        lengths,
        slopes,
    )
    attended_req = attended.reshape(requests, slot, local_heads * HD)
    local_ids = lax.dynamic_slice_in_dim(adapter_ids, req_index * requests, requests)
    every_down, every_up = (
        lax.all_gather(adapter_down, "req", axis=0, tiled=True),
        lax.all_gather(adapter_up, "req", axis=0, tiled=True),
    )
    table_rows = adapter_rows[local_ids]
    pick = (table_rows[:, None] == jnp.arange(ADAPTERS, dtype=jnp.int32)[None, :]).astype(
        jnp.bfloat16
    )
    chosen_down = jnp.einsum(
        "ra,akd->rkd", pick, every_down, preferred_element_type=jnp.float32
    ).astype(jnp.bfloat16)
    chosen_up = jnp.einsum(
        "ra,akd->rkd", pick, every_up, preferred_element_type=jnp.float32
    ).astype(jnp.bfloat16)
    dense_part = jnp.dot(
        attended.reshape(requests * slot, local_heads * HD),
        dense_weight,
        preferred_element_type=jnp.float32,
    )
    low_part = jnp.einsum(
        "rsd,rkd->rsk", attended_req, chosen_down, preferred_element_type=jnp.float32
    )
    low_part = low_part.reshape(requests * slot, low_part.shape[2])
    dense, low = (
        lax.psum_scatter(
            dense_part.astype(jnp.bfloat16), "mlp", scatter_dimension=0, tiled=True
        ).astype(jnp.float32),
        lax.psum_scatter(
            low_part.astype(jnp.bfloat16), "mlp", scatter_dimension=0, tiled=True
        ).astype(jnp.float32),
    )
    low = low.astype(jnp.bfloat16).reshape(own_requests, slot, low.shape[1])
    own_up = lax.dynamic_slice_in_dim(chosen_up, mlp_index * own_requests, own_requests)
    delta = jnp.einsum("rsk,rkd->rsd", low, own_up, preferred_element_type=jnp.float32).reshape(
        row_share, tokens.shape[1]
    )
    own_tokens = lax.dynamic_slice_in_dim(tokens, mlp_index * row_share, row_share)
    residual = (own_tokens.astype(jnp.float32) + dense + delta).astype(jnp.bfloat16)
    normed_two = layer_norm(residual, second_gain)
    expanded = gelu_tanh(
        jnp.dot(
            lax.all_gather(normed_two, "mlp", axis=0, tiled=True),
            up_weight,
            preferred_element_type=jnp.float32,
        )
    ).astype(jnp.bfloat16)
    feed = lax.psum_scatter(
        jnp.dot(expanded, down_weight, preferred_element_type=jnp.float32).astype(jnp.bfloat16),
        "mlp",
        scatter_dimension=0,
        tiled=True,
    ).astype(jnp.float32)
    own_valid = lax.dynamic_slice_in_dim(valid.reshape(-1), mlp_index * row_share, row_share)
    layer_out = jnp.where(
        own_valid[:, None], residual.astype(jnp.float32) + feed, jnp.zeros((), jnp.float32)
    ).astype(jnp.bfloat16)
    flat = fresh.reshape(requests, -1)
    moving = flat[migrants]
    own_slots = req_index * requests + jnp.arange(requests, dtype=jnp.int32)
    lands_here = landing[None, :] == own_slots[:, None]
    arrived = lax.all_gather(moving, "req", axis=0, tiled=True)
    matching = lands_here.astype(jnp.bfloat16)
    picked = jnp.dot(matching, arrived, preferred_element_type=jnp.float32).astype(jnp.bfloat16)
    moved_in = jnp.any(lands_here, axis=1)
    page_out = jnp.where(moved_in[:, None], picked, flat).reshape(
        requests, slot, flat.shape[1] // slot
    )
    return (layer_out, page_out)


def solution(mesh):
    return jax.shard_map(
        shards,
        mesh=mesh,
        in_specs=(
            P("req", None),
            P(),
            P(None, "mlp"),
            P("mlp", None),
            P("req", None, "mlp"),
            P("req", None, None),
            P(),
            P(),
            P(),
            P(None, "mlp"),
            P("mlp", None),
            P("req", None, "mlp"),
            P("req", None),
            P("req"),
            P("req"),
            P("req"),
            P(),
        ),
        out_specs=(P(("req", "mlp"), None), P("req", None, "mlp")),
        check_vma=False,
    )
```

profile of v0, /device:TPU:0, one launch (start us, length us, event | category | flops | bytes accessed | tf_op | source)
XLA Modules:
  0.0 414.1 jit_solution(13141839488661226684)
XLA Ops:
  9.1 2.2 copy.129
  13.4 3.0 convert_reduce_fusion
  18.1 10.7 %fusion.30 = bf16[1024,1536]{1,0:T(8,128)(2,1)} fusion(bf16[2048,1536]{1,0:T(8,128)(2,1)} %param.19, bf16[1024,2048]{1,0:T(8,128)(2,1)S(1)} %copy-done.4, f32[2048]{0:T(1024)S(1)} %copy-done.12, f32[1024]{0:T(1024)S(1)} %add_rsqrt_fusion, f32[1024]{0:T(1024)S(1)} %broadcast_multiply_fusion.2), kind=kOutput, calls=%fused_computation.39 | convolution fusion | flops 6454509568 | bytes 13647872 | tf_op jit(solution)/shard_map/dot_general | solution.py:89
  28.9 4.6 %copy.112 = bf16[12,128,1024]{1,2,0:T(8,128)(2,1)} copy(bf16[12,128,1024]{2,1,0:T(8,128)(2,1)} %param.28) | data formatting | bytes 6291456 | tf_op args[11]
  33.6 4.6 %copy.115 = bf16[12,128,4,2,128]{4,1,3,2,0:T(8,128)(2,1)} copy(bf16[12,128,4,2,128]{1,4,3,2,0:T(8,128)(2,1)} %bitcast.87) | data formatting | bytes 6291456 | tf_op jit(solution)/shard_map/reshape | solution.py:95
  38.2 6.8 %gather_fusion.1 = bf16[32,128,4,2,128]{4,1,3,2,0:T(8,128)(2,1)} fusion(bf16[12,128,4,2,128]{4,1,3,2,0:T(8,128)(2,1)} %copy.115, s32[1024]{0:T(1024)S(1)} %pad_clamp_fusion.2), kind=kCustom, calls=%fused_computation.1 | custom fusion | bytes 16777344 | tf_op jit(solution)/shard_map/gather | solution.py:96
  45.0 10.4 %copy.116 = bf16[32,128,4,2,128]{4,1,0,3,2:T(8,128)(2,1)} copy(bf16[32,128,4,2,128]{4,1,3,2,0:T(8,128)(2,1)} %gather_fusion.1) | data formatting | bytes 16777216 | tf_op jit(solution)/shard_map/gather | solution.py:96
  55.4 4.7 %copy.118 = bf16[1024,1536]{0,1:T(8,128)(2,1)} copy(bf16[1024,1536]{1,0:T(8,128)(2,1)} %fusion.30) | data formatting | bytes 6291456 | tf_op jit(solution)/shard_map/convert_element_type | solution.py:89
  60.1 2.9 copy.144
  68.3 2.4 copy.140
  70.7 5.9 %fusion.70 = (bf16[8,512,4,1,128]{4,1,0,3,2:T(8,128)(2,1)}, bf16[8,512,4,1,128]{4,1,0,3,2:T(8,128)(2,1)}) fusion(bf16[8,512,4,2,128]{4,1,0,3,2:T(8,128)(2,1)} %bitcast.83), kind=kLoop, calls=%fused_computation.116 | loop fusion | bytes 16777216 | tf_op jit(solution)/shard_map/slice | solution.py:107
  76.6 6.4 %copy.137 = bf16[8,512,4,1,128]{1,4,2,0,3:T(8,128)(2,1)} copy(bf16[8,512,4,1,128]{4,1,0,3,2:T(8,128)(2,1)} %get-tuple-element.17) | data formatting | bytes 8388608
  83.8 2.5 fusion.73
  88.2 2.5 fusion.12
  90.8 3.5 fusion.18
  99.9 5.6 %convolution_convert_fusion.1 = bf16[1024,2048]{1,0:T(8,128)(2,1)} fusion(bf16[512,2048]{1,0:T(8,128)(2,1)S(1)} %copy-done, bf16[64,8,8,128]{3,2,1,0:T(8,128)(2,1)} %bitcast.93), kind=kOutput, calls=%fused_computation.40 | convolution fusion | flops 2149580800 | bytes 7340032 | tf_op jit(solution)/shard_map/dot_general | solution.py:128
  107.5 3.2 copy.133
  116.1 1.8 gather_fusion.4
  118.0 8.8 %all-gather.8.cloned.1.call-done = bf16[64,16,2048]{2,0,1:T(8,128)(2,1)} async-done(((bf16[8,16,2048]{2,0,1:T(8,128)(2,1)}), bf16[64,16,2048]{2,0,1:T(8,128)(2,1)}) %all-gather.8.cloned.1.call-update) | async-done | bytes 4194320 | tf_op jit(solution)/shard_map/all_gather | solution.py:116
  126.8 2.9 fusion.56
  129.9 17.0 %reduce-scatter.6.cloned.1.call-done = bf16[256,16]{0,1:T(8,128)(2,1)} async-done(((bf16[1024,16]{0,1:T(8,128)(2,1)}), bf16[256,16]{0,1:T(8,128)(2,1)}) %reduce-scatter.6.cloned.1.call-update) | async-done | bytes 8208 | tf_op jit(solution)/shard_map/reduce_scatter | solution.py:141
  148.0 45.9 %reduce-scatter.4.cloned.1.call-done = bf16[256,2048]{1,0:T(8,128)(2,1)} async-done(((bf16[1024,2048]{1,0:T(8,128)(2,1)}), bf16[256,2048]{1,0:T(8,128)(2,1)}) %reduce-scatter.4.cloned.1.call-update) | async-done | bytes 1048592 | tf_op jit(solution)/shard_map/reduce_scatter | solution.py:138
  193.9 2.2 convert_reduce_fusion.1
  198.0 2.7 maximum_bitcast_fusion
  200.8 31.8 %all-gather.10.cloned.1.call-done = bf16[1024,2048]{1,0:T(8,128)(2,1)} async-done(((bf16[256,2048]{1,0:T(8,128)(2,1)}), bf16[1024,2048]{1,0:T(8,128)(2,1)}) %all-gather.10.cloned.1.call-update) | async-done | bytes 4194320 | tf_op jit(solution)/shard_map/all_gather | solution.py:155
  232.6 25.4 %fusion.27 = bf16[1024,2048]{1,0:T(8,128)(2,1)} fusion(bf16[2048,2048]{1,0:T(8,128)(2,1)} %param.27, bf16[1024,2048]{1,0:T(8,128)(2,1)} %all-gather.10.cloned.1.call-done, bf16[2048,2048]{1,0:T(8,128)(2,1)} %param.26), kind=kOutput, calls=%fused_computation.38 | convolution fusion | flops 17200840704 | bytes 25165824 | tf_op jit(solution)/shard_map/dot_general | solution.py:161
  258.8 100.6 %all-gather.12.cloned.1.call-done = bf16[8,4,131072]{2,1,0:T(4,128)(2,1)} async-done(((bf16[1,4,131072]{2,1,0:T(4,128)(2,1)}), bf16[8,4,131072]{2,1,0:T(4,128)(2,1)}) %all-gather.12.cloned.1.call-update) | async-done | bytes 8388624 | tf_op jit(solution)/shard_map/all_gather | solution.py:174
  359.5 7.7 %reshape.302 = bf16[32,131072]{1,0:T(8,128)(2,1)} reshape(bf16[8,4,131072]{2,1,0:T(4,128)(2,1)} %all-gather.12.cloned.1.call-done) | data formatting | bytes 16777216
  367.2 6.7 %fusion = bf16[8,131072]{1,0:T(8,128)(2,1)S(1)} fusion(bf16[8,131072]{1,0:T(8,128)(2,1)} %copy-done.5, bf16[32,131072]{1,0:T(8,128)(2,1)} %reshape.302, pred[8]{0:T(512)(128)(4,1)S(1)} %compare_reduce_fusion, s32[32]{0:T(128)S(1)} %copy-done.10, s32[8]{0:T(128)S(1)} %iota_add_fusion), kind=kOutput, calls=%fused_computation.6 | convolution fusion | flops 69206272 | bytes 12583080 | tf_op jit(solution)/shard_map/dot_general | solution.py:176
  373.9 2.5 copy.134
  376.4 28.3 %reduce-scatter.8.cloned.1.call-done = bf16[256,2048]{1,0:T(8,128)(2,1)} async-done(((bf16[1024,2048]{1,0:T(8,128)(2,1)}), bf16[256,2048]{1,0:T(8,128)(2,1)}) %reduce-scatter.8.cloned.1.call-update) | async-done | bytes 1048592 | tf_op jit(solution)/shard_map/reduce_scatter | solution.py:160
  404.7 2.5 fusion.39
  (96 shorter events, 30.7 us)
Async XLA Ops:
  7.2 92.8 %copy-start = (bf16[512,2048]{1,0:T(8,128)(2,1)S(1)}, bf16[512,2048]{1,0:T(8,128)(2,1)}, u32[]{:S(2)}) copy-start(bf16[512,2048]{1,0:T(8,128)(2,1)} %param.20) | copy-start | bytes 6291460
  7.2 90.2 %all-gather.6.cloned.1.call-start = ((), (), s32[]{:S(2)}) async-start(), calls=%async_computation.4 | async-start | bytes 1179648 | tf_op jit(solution)/shard_map/all_gather | solution.py:115
  9.0 117.8 %all-gather.8.cloned.1.call-start = ((), (), s32[]{:S(2)}) async-start(), calls=%async_computation.6 | async-start | bytes 4718592 | tf_op jit(solution)/shard_map/all_gather | solution.py:116
  11.3 135.6 %reduce-scatter.6.cloned.1.call-start = ((), (), s32[]{:S(2)}) async-start(), calls=%async_computation.5 | async-start | bytes 40960 | tf_op jit(solution)/shard_map/reduce_scatter | solution.py:141
  13.4 3.4 copy-start.4
  13.4 4.7 %copy-start.12 = (f32[2048]{0:T(1024)S(1)}, f32[2048]{0:T(1024)}, u32[]{:S(2)}) copy-start(f32[2048]{0:T(1024)} %param.18) | copy-start | bytes 24580
  63.0 1.7 copy-start.3
  76.6 6.5 %copy-start.11 = (s32[8]{0:T(128)S(1)}, s32[8]{0:T(128)}, u32[]{:S(2)}) copy-start(s32[8]{0:T(128)} %param.31) | copy-start | bytes 100
  83.0 3.3 copy-start.6
  88.2 2.5 copy-start.7
  90.8 3.5 copy-start.8
  94.3 2.5 copy-start.2
  99.9 94.1 %reduce-scatter.4.cloned.1.call-start = ((), (), s32[]{:S(2)}) async-start(), calls=%async_computation.3 | async-start | bytes 5242880 | tf_op jit(solution)/shard_map/reduce_scatter | solution.py:138
  105.5 127.1 %all-gather.10.cloned.1.call-start = ((), (), s32[]{:S(2)}) async-start(), calls=%async_computation.7 | async-start | bytes 5242880 | tf_op jit(solution)/shard_map/all_gather | solution.py:155
  105.6 5.1 %copy-start.13 = (s32[4]{0:T(128)S(1)}, s32[4]{0:T(128)}, u32[]{:S(2)}) copy-start(s32[4]{0:T(128)} %param.32) | copy-start | bytes 52
  112.9 1.3 copy-start.5
  129.9 66.7 %copy-start.9 = (f32[2048]{0:T(1024)S(1)}, f32[2048]{0:T(1024)}, u32[]{:S(2)}) copy-start(f32[2048]{0:T(1024)} %param.25) | copy-start | bytes 24580
  198.0 161.5 %all-gather.12.cloned.1.call-start = ((), (), s32[]{:S(2)}) async-start(), calls=%async_computation.9 | async-start | bytes 9437184 | tf_op jit(solution)/shard_map/all_gather | solution.py:174
  200.7 204.0 %reduce-scatter.8.cloned.1.call-start = ((), (), s32[]{:S(2)}) async-start(), calls=%async_computation.8 | async-start | bytes 5242880 | tf_op jit(solution)/shard_map/reduce_scatter | solution.py:160
  258.0 0.7 copy-start.10
  367.2 40.0 %copy-start.1 = (bf16[512,2048]{1,0:T(8,128)(2,1)S(1)}, bf16[512,2048]{1,0:T(8,128)(2,1)}, u32[]{:S(2)}) copy-start(bf16[512,2048]{1,0:T(8,128)(2,1)} %param.20) | copy-start | bytes 6291460
Sparse Core Ops, SparseCore 0:
  10.1 42.2 all-gather.5
  54.5 72.2 all-gather.7
  129.2 17.6 reduce-scatter.5
  149.4 44.4 reduce-scatter.3
  198.1 34.4 all-gather.9
  234.6 124.8 all-gather.11
  362.0 42.6 reduce-scatter.7
where the time goes:
time: 415 us; the launch traced here: 414 us
  waiting for transfers between devices  233 us (56%)
  local copies, waits for them, and re-layouts  84.5 us (20%)
  matrix products  62.4 us (15%)
  other arithmetic  19.8 us (5%)
  between operations  14.5 us (3%)
    all_gather x1, waiting for transfers between devices, shards(): arrived = lax.all_gather(moving, 'req', axis=0, tiled=True)  101 us
    reduce_scatter x1, waiting for transfers between devices, shards(): lax.psum_scatter(dense_part.astype(jnp.bfloat16), 'mlp', scatter_dimensio...  45.9 us
    unnamed x37, local copies, waits for them, and re-layouts  36.4 us
    all_gather x1, waiting for transfers between devices, shards(): lax.all_gather(normed_two, 'mlp', axis=0, tiled=True)  31.8 us
    reduce_scatter x1, waiting for transfers between devices, shards(): lax.psum_scatter(jnp.dot(expanded, down_weight, preferred_element_type=jn...  28.3 us
    dot_general x1, matrix products, shards(): jnp.dot(expanded, down_weight, preferred_element_type=jnp.float32)  25.4 us
    gather x2, local copies, waits for them, and re-layouts, shards(): pool_view[pages]  17.1 us
    reduce_scatter x1, waiting for transfers between devices, shards(): lax.psum_scatter(low_part.astype(jnp.bfloat16), 'mlp', scatter_dimension=...  17 us
  transfers between devices with their start and end apart: 7, of which 6 were waited for; matrix products, arithmetic and copies ran while one was open for 37% of the time, Pallas kernels for 0%

commit v1 on v0

v1 whole, which is shorter than its diff:
```python
import functools
import math

import jax
import jax.numpy as jnp
from jax import lax
from jax.experimental import pallas as pl
from jax.experimental.pallas import tpu as pltpu
from jax.sharding import PartitionSpec as P

HEADS = 16
HD = 128
ADAPTERS = 64
CORES = 2


EPS = 1e-05


def layer_norm(values, gain):
    values = values.astype(jnp.float32)
    mean = jnp.mean(values, axis=-1, keepdims=True)
    centred = values - mean
    variance = jnp.mean(centred * centred, axis=-1, keepdims=True)
    return (centred * lax.rsqrt(variance + EPS) * gain).astype(jnp.bfloat16)


def gelu_tanh(value):
    return 0.5 * value * (1.0 + jnp.tanh(0.7978845608 * (value + 0.044715 * value * value * value)))


def attend_body(local_heads, n_pages, order, pages, lens, slopes, joined, *refs):
    page_refs = refs[:n_pages]
    dense_w = refs[n_pages]
    attended, fresh, dense = refs[n_pages + 1 :]
    request = order[pl.program_id(0)]
    length = lens[request]
    slot = joined.shape[0]
    pre_len = n_pages * page_refs[0].shape[1]
    total_len = pre_len + slot
    scale = 1.0 / math.sqrt(HD)
    row = lax.broadcasted_iota(jnp.int32, (slot, total_len), 0)
    col = lax.broadcasted_iota(jnp.int32, (slot, total_len), 1)
    distance = (pre_len + row - col).astype(jnp.float32)
    allowed = (col < pre_len) | ((col - pre_len <= row) & (col - pre_len < length))
    valid = lax.broadcasted_iota(jnp.int32, (slot, 2 * HD), 0) < length
    for h in range(local_heads):
        base = h * 3 * HD
        query = joined[:, base : base + HD]
        own = joined[:, base + HD : base + 3 * HD]
        fresh[0, :, h * 2 * HD : (h + 1) * 2 * HD] = jnp.where(
            valid, own, jnp.zeros((), jnp.bfloat16)
        )
        keys = jnp.concatenate(
            [p[0, :, h * 2 * HD : h * 2 * HD + HD] for p in page_refs] + [own[:, :HD]], axis=0
        )
        values = jnp.concatenate(
            [p[0, :, h * 2 * HD + HD : (h + 1) * 2 * HD] for p in page_refs] + [own[:, HD:]],
            axis=0,
        )
        scores = lax.dot_general(
            query, keys, (((1,), (1,)), ((), ())), preferred_element_type=jnp.float32
        )
        scores = jnp.where(allowed, scores * scale - slopes[h] * distance, -jnp.inf)
        top = jnp.max(scores, axis=-1, keepdims=True)
        weights = jnp.exp(scores - top)
        total = jnp.sum(weights, axis=-1, keepdims=True)
        weights = (weights / total).astype(jnp.bfloat16)
        mixed = jnp.dot(weights, values, preferred_element_type=jnp.float32)
        attended[:, h * HD : (h + 1) * HD] = mixed.astype(jnp.bfloat16)
    dense[...] = jnp.dot(
        attended[...], dense_w[...], preferred_element_type=jnp.float32
    ).astype(jnp.bfloat16)


def attend(joined, pool, pages, lens, slopes, order, dense_weight, slot):
    count = order.shape[0]
    n_pages = pages.shape[1]
    width = joined.shape[1]
    local_heads = width // (3 * HD)
    page_specs = [
        pl.BlockSpec(
            (1, pool.shape[1], pool.shape[2]),
            functools.partial(lambda p, i, o, pg, ln, sl: (pg[o[i], p], 0, 0), p),
        )
        for p in range(n_pages)
    ]
    return pl.pallas_call(
        functools.partial(attend_body, local_heads, n_pages),
        grid_spec=pltpu.PrefetchScalarGridSpec(
            num_scalar_prefetch=4,
            grid=(count,),
            in_specs=[pl.BlockSpec((slot, width), lambda i, o, pg, ln, sl: (o[i], 0))]
            + page_specs
            + [pl.BlockSpec(dense_weight.shape, lambda i, o, pg, ln, sl: (0, 0))],
            out_specs=[
                pl.BlockSpec((slot, local_heads * HD), lambda i, o, pg, ln, sl: (i, 0)),
                pl.BlockSpec((1, slot, local_heads * 2 * HD), lambda i, o, pg, ln, sl: (i, 0, 0)),
                pl.BlockSpec((slot, dense_weight.shape[1]), lambda i, o, pg, ln, sl: (i, 0)),
            ],
        ),
        out_shape=[
            jax.ShapeDtypeStruct((count * slot, local_heads * HD), jnp.bfloat16),
            jax.ShapeDtypeStruct((count, slot, local_heads * 2 * HD), jnp.bfloat16),
            jax.ShapeDtypeStruct((count * slot, dense_weight.shape[1]), jnp.bfloat16),
        ],
        compiler_params=pltpu.CompilerParams(vmem_limit_bytes=40 * 1024 * 1024),
        cost_estimate=pl.CostEstimate(
            flops=6 * 10**9 * count // 8, bytes_accessed=2 * 10**7 * count // 8, transcendentals=0
        ),
    )(order, pages, lens, slopes, joined, *([pool] * n_pages), dense_weight)


def merge_body(source, came, fresh, arrived, out):
    here = came[pl.program_id(0)]

    @pl.when(here == 0)
    def _():
        out[...] = fresh[...]

    @pl.when(here != 0)
    def _():
        out[...] = arrived[...]


def merge(fresh, place, arrived, source, came):
    requests = came.shape[0]
    block = (1,) + fresh.shape[1:]
    return pl.pallas_call(
        lambda place, source, came, *refs: merge_body(source, came, *refs),
        grid_spec=pltpu.PrefetchScalarGridSpec(
            num_scalar_prefetch=3,
            grid=(requests,),
            in_specs=[
                pl.BlockSpec(block, lambda i, p, s, c: (p[i], 0, 0)),
                pl.BlockSpec(block, lambda i, p, s, c: (s[i], 0, 0)),
            ],
            out_specs=pl.BlockSpec(block, lambda i, p, s, c: (i, 0, 0)),
        ),
        out_shape=jax.ShapeDtypeStruct(fresh.shape, fresh.dtype),
    )(place, source, came, fresh, arrived)


def shards(
    tokens,
    first_gain,
    joined_weight,
    dense_weight,
    adapter_down,
    adapter_up,
    adapter_ids,
    adapter_rows,
    second_gain,
    up_weight,
    down_weight,
    page_pool,
    page_table,
    group_index,
    lengths,
    migrants,
    landing,
):
    mlp_count = lax.axis_size("mlp")
    req_count = lax.axis_size("req")
    req_index = lax.axis_index("req")
    mlp_index = lax.axis_index("mlp")
    requests = lengths.shape[0]
    slot = tokens.shape[0] // requests
    width = tokens.shape[1]
    local_heads = joined_weight.shape[1] // (3 * HD)
    own_requests = requests // mlp_count
    rows = mlp_count // CORES
    row_index = mlp_index // CORES
    core_index = mlp_index % CORES
    core_pairs = [(m, m ^ 1) for m in range(mlp_count)]

    def across_rows(values):
        out = [values]
        for k in range(1, rows):
            pairs = [(m, (m + k * CORES) % mlp_count) for m in range(mlp_count)]
            out.append(lax.ppermute(values, "mlp", pairs))
        return out

    local_ids = lax.dynamic_slice_in_dim(adapter_ids, req_index * requests, requests)
    table_rows = adapter_rows[local_ids]
    cols = adapter_down.shape[2]
    own_up = lax.dynamic_slice_in_dim(adapter_up, mlp_index * cols, cols, axis=2)
    tables = lax.all_gather(
        jnp.concatenate([adapter_down, own_up], axis=2), "req", axis=0, tiled=True
    )
    chosen = tables[table_rows]
    chosen_down = chosen[:, :, :cols]
    chosen_up = lax.all_gather(chosen[:, :, cols:], "mlp", axis=2, tiled=True)

    normed = layer_norm(tokens, first_gain)
    joined = jnp.dot(normed, joined_weight, preferred_element_type=jnp.float32).astype(jnp.bfloat16)
    pages = page_table[group_index]
    head_pos = (mlp_index * local_heads + jnp.arange(local_heads, dtype=jnp.int32)).astype(
        jnp.float32
    )
    slopes = jnp.exp2(-8.0 * (head_pos + 1.0) / HEADS)

    grid_rows = jnp.arange(rows, dtype=jnp.int32)[None, :]
    grid_cores = (jnp.arange(CORES, dtype=jnp.int32)[:, None] + core_index) % CORES
    orders = [
        ((grid_rows * CORES + grid_cores) * own_requests + c).reshape(-1)
        for c in range(own_requests)
    ]
    half = rows * slot
    firsts = []
    freshes = []
    for c in range(own_requests):
        attended, fresh_c, dense_part = attend(
            joined, page_pool, pages, lengths, slopes, orders[c], dense_weight, slot
        )
        freshes.append(fresh_c)
        firsts.append((attended, dense_part))
    fresh = jnp.concatenate(freshes, axis=0)
    order = jnp.concatenate(orders)
    place = jnp.argmax(
        (order[None, :] == jnp.arange(requests, dtype=jnp.int32)[:, None]).astype(jnp.int32), axis=1
    ).astype(jnp.int32)

    outs = []
    for c in range(own_requests):
        attended, dense_part = firsts[c]
        low_part = lax.dot_general(
            chosen_down[orders[c]],
            attended.reshape(mlp_count, slot, local_heads * HD),
            (((2,), (2,)), ((0,), (0,))),
            preferred_element_type=jnp.float32,
        ).astype(jnp.bfloat16)
        in_order = jnp.arange(mlp_count, dtype=jnp.int32) // CORES
        swap = in_order + (
            (jnp.arange(mlp_count, dtype=jnp.int32) % CORES + core_index) % CORES
        ) * rows
        every_low = lax.all_gather(low_part[swap], "mlp", axis=0, tiled=False)
        low_all = jnp.sum(every_low.astype(jnp.float32), axis=0).astype(jnp.bfloat16)
        mine = orders[c][:rows]
        low = low_all.reshape(rows, CORES, low_all.shape[1], slot)
        low = lax.dynamic_index_in_dim(low, core_index, axis=1, keepdims=False)
        delta = lax.dot_general(
            low,
            chosen_up[mine],
            (((1,), (1,)), ((0,), (0,))),
            preferred_element_type=jnp.float32,
        ).reshape(half, width)
        other = lax.ppermute(dense_part[half:], "mlp", core_pairs)
        pair_sum = (dense_part[:half].astype(jnp.float32) + other.astype(jnp.float32)).astype(
            jnp.bfloat16
        )
        dense = sum(part.astype(jnp.float32) for part in across_rows(pair_sum))
        own_tokens = tokens.reshape(rows, CORES, own_requests, slot, width)[:, :, c]
        own_tokens = lax.dynamic_index_in_dim(own_tokens, core_index, axis=1, keepdims=False)
        residual = (
            own_tokens.reshape(half, width).astype(jnp.float32) + dense + delta
        ).astype(jnp.bfloat16)
        normed_two = layer_norm(residual, second_gain)
        theirs = lax.ppermute(normed_two, "mlp", core_pairs)
        expanded = gelu_tanh(
            jnp.dot(
                jnp.concatenate([normed_two, theirs], axis=0),
                up_weight,
                preferred_element_type=jnp.float32,
            )
        ).astype(jnp.bfloat16)
        part = jnp.dot(expanded, down_weight, preferred_element_type=jnp.float32).astype(
            jnp.bfloat16
        )
        other = lax.ppermute(part[half:], "mlp", core_pairs)
        pair_sum = (part[:half].astype(jnp.float32) + other.astype(jnp.float32)).astype(
            jnp.bfloat16
        ).reshape(rows, slot, width)
        feed = lax.dynamic_index_in_dim(pair_sum, row_index, axis=0, keepdims=False).astype(
            jnp.float32
        )
        for k in range(1, rows):
            pairs = [(m, (m + k * CORES) % mlp_count) for m in range(mlp_count)]
            send = lax.dynamic_index_in_dim(
                pair_sum, (row_index + k) % rows, axis=0, keepdims=False
            )
            feed = feed + lax.ppermute(send, "mlp", pairs).astype(jnp.float32)
        own_res = lax.dynamic_index_in_dim(
            residual.reshape(rows, slot, width), row_index, axis=0, keepdims=False
        )
        length = lengths[mlp_index * own_requests + c]
        own_valid = jnp.arange(slot, dtype=jnp.int32) < length
        outs.append(
            jnp.where(
                own_valid[:, None], own_res.astype(jnp.float32) + feed, jnp.zeros((), jnp.float32)
            ).astype(jnp.bfloat16)
        )
    layer_out = jnp.concatenate(outs, axis=0)

    moves = migrants.shape[0]
    my_landing = lax.dynamic_slice_in_dim(landing, req_index * moves, moves)
    own_slots = req_index * requests + jnp.arange(requests, dtype=jnp.int32)
    lands_here = landing[None, :] == own_slots[:, None]
    came = jnp.any(lands_here, axis=1).astype(jnp.int32)
    owner = jnp.argmax(lands_here.astype(jnp.int32), axis=1).astype(jnp.int32) // moves
    arrived = []
    for k in range(1, req_count):
        to = (req_index + k) % req_count
        hit = (my_landing // requests == to).astype(jnp.int32)
        send = lax.dynamic_index_in_dim(
            fresh, place[jnp.sum(hit * migrants)], axis=0, keepdims=True
        )
        pairs = [(r, (r + k) % req_count) for r in range(req_count)]
        arrived.append(lax.ppermute(send, "req", pairs))
    arrived = jnp.concatenate(arrived, axis=0)
    source = jnp.where(came > 0, (req_index - owner - 1) % req_count, 0).astype(jnp.int32)
    source = jnp.clip(source, 0, req_count - 2)
    page_out = merge(fresh, place, arrived, source, came)
    return (layer_out, page_out)


def solution(mesh):
    return jax.shard_map(
        shards,
        mesh=mesh,
        in_specs=(
            P("req", None),
            P(),
            P(None, "mlp"),
            P("mlp", None),
            P("req", None, "mlp"),
            P("req", None, None),
            P(),
            P(),
            P(),
            P(None, "mlp"),
            P("mlp", None),
            P("req", None, "mlp"),
            P("req", None),
            P("req"),
            P("req"),
            P("req"),
            P(),
        ),
        out_specs=(P(("req", "mlp"), None), P("req", None, "mlp")),
        check_vma=False,
    )
```

time: 415 us -> 265 us (0.64)
  waiting for transfers between devices: 233 us -> 12.4 us
  blocking collectives: 0 us -> 47.2 us
  local copies, waits for them, and re-layouts: 84.5 us -> 42.1 us
  between operations: 14.5 us -> 40.3 us
  Pallas kernels: 0 us -> 25.4 us
  starting transfers between devices: 0.29 us -> 20.6 us
  matrix products: 62.4 us -> 45.4 us
  other arithmetic: 19.8 us -> 30.8 us
    all_gather x4 -> x1, waiting for transfers between devices: 141 us -> 0.01 us  [shards(): lax.all_gather(jnp.concatenate([adapter_down, own_up], axis=2), 'req', ax...]
    reduce_scatter x3 -> x0, waiting for transfers between devices: 91.2 us -> none  [the longest x1 45.9 us: shards(): lax.psum_scatter(dense_part.astype(jnp.bfloat16), 'mlp', scatter_dimensio...]
    all_gather x0 -> x3, blocking collectives: none -> 47.2 us  [the longest x2 26.8 us: shards(): every_low = lax.all_gather(low_part[swap], 'mlp', axis=0, tiled=False)]
    pallas_call x0 -> x3, Pallas kernels: none -> 25.4 us  [the longest x2 18.7 us: attend(): pl.pallas_call(functools.partial(attend_body, local_heads, n_pages), grid...]
    dot_general x10 -> x4, matrix products: 26.3 us -> 1.42 us  [the longest x2 0.95 us: shards(): lax.dot_general(low, chosen_up[mine], (((1,), (1,)), ((0,), (0,))), prefe...]
    unnamed x37 -> x65, local copies, waits for them, and re-layouts: 36.4 us -> 14.1 us
    ppermute x0 -> x17, starting transfers between devices: none -> 20.6 us  [the longest x7 13.8 us: shards(): arrived.append(lax.ppermute(send, 'req', pairs))]
    gather x5 -> x7, local copies, waits for them, and re-layouts: 20.9 us -> 5.52 us  [the longest x1 2.15 us: shards(): chosen = tables[table_rows]]
  transfers between devices with their start and end apart: 7 -> 18, of which waited for: 6 -> 2; matrix products, arithmetic and copies ran while one was open for 37% -> 41% of each run, Pallas kernels for 0% -> 10%
where the time goes in v1:
time: 265 us; the launch traced here: 264 us
  blocking collectives  47.2 us (18%)
  matrix products  45.4 us (17%)
  local copies, waits for them, and re-layouts  42.1 us (16%)
  between operations  40.3 us (15%)
  other arithmetic  30.8 us (12%)
  Pallas kernels  25.4 us (10%)
  starting transfers between devices  20.6 us (8%)
  waiting for transfers between devices  12.4 us (5%)
    dot_general x2, matrix products, shards(): jnp.dot(expanded, down_weight, preferred_element_type=jnp.float32)  33.4 us
    all_gather x2, blocking collectives, shards(): every_low = lax.all_gather(low_part[swap], 'mlp', axis=0, tiled=False)  26.8 us
    all_gather x1, blocking collectives, shards(): chosen_up = lax.all_gather(chosen[:, :, cols:], 'mlp', axis=2, tiled=True)  20.5 us
    pallas_call x2, Pallas kernels, attend(): pl.pallas_call(functools.partial(attend_body, local_heads, n_pages), grid...  18.7 us
    unnamed x65, local copies, waits for them, and re-layouts  14.1 us
    ppermute x7, starting transfers between devices, shards(): arrived.append(lax.ppermute(send, 'req', pairs))  13.8 us
    ppermute x2, waiting for transfers between devices, shards(): feed = feed + lax.ppermute(send, 'mlp', pairs).astype(jnp.float32)  12.3 us
    dot_general x1, matrix products, shards(): jnp.dot(normed, joined_weight, preferred_element_type=jnp.float32)  10.6 us
  transfers between devices with their start and end apart: 18, of which 2 were waited for; matrix products, arithmetic and copies ran while one was open for 41% of the time, Pallas kernels for 10%

profile of v1, /device:TPU:0, one launch (start us, length us, event | category | flops | bytes accessed | tf_op | source)
XLA Modules:
  0.0 264.2 jit_solution(15680621498400510028)
XLA Ops:
  8.2 1.6 pad_maximum_fusion.1
  10.8 3.0 %convert_reduce_fusion = f32[1024]{0:T(1024)S(1)} fusion(bf16[1024,2048]{1,0:T(8,128)(2,1)} %param.17), kind=kLoop, calls=%fused_computation.10 | loop fusion | flops 4193280 | bytes 4198400 | tf_op jit(solution)/shard_map/reduce_sum | solution.py:22
  16.1 10.6 %fusion.20.joined = bf16[1024,1536]{1,0:T(8,128)(2,1)S(1)} fusion(bf16[2048,1536]{1,0:T(8,128)(2,1)} %param.19, bf16[1024,2048]{1,0:T(8,128)(2,1)} %param.17, f32[2048]{0:T(1024)S(1)} %copy-done.28, f32[1024]{0:T(1024)S(1)} %add_rsqrt_fusion, f32[1024]{0:T(1024)S(1)} %broadcast_multiply_fusion), kind=kOutput, calls=%fused_computation.32 | convolution fusion | flops 6454509568 | bytes 13647872 | tf_op jit(solution)/shard_map/dot_general | solution.py:196
  26.8 9.3 %shard_map.176 = (bf16[512,512]{1,0:T(8,128)(2,1)S(1)}, bf16[4,128,1024]{2,1,0:T(8,128)(2,1)S(1)}, bf16[512,2048]{1,0:T(8,128)(2,1)S(1)}) custom-call(s32[4]{0:T(128)S(1)} %mul.176.order, s32[8,4]{1,0:T(8,128)S(1)} %gather_fusion, s32[8]{0:T(128)S(1)} %copy-done.12, f32[4]{0:T(128)S(1)} %multiply_exponential_fusion.slopes, ...), custom_call_target="tpu_custom_call" | custom-call | flops 3000000000 | bytes 10000000 | tf_op jit(solution)/shard_map/pallas_call | solution.py:88
  37.7 9.3 %shard_map.177 = (bf16[512,512]{1,0:T(8,128)(2,1)S(1)}, bf16[4,128,1024]{2,1,0:T(8,128)(2,1)S(1)}, bf16[512,2048]{1,0:T(8,128)(2,1)S(1)}) custom-call(s32[4]{0:T(128)S(1)} %broadcast_add_fusion.1.order, s32[8,4]{1,0:T(8,128)S(1)} %gather_fusion, s32[8]{0:T(128)S(1)} %copy-done.12, f32[4]{0:T(128)S(1)} %multiply_exponential_fusion.slopes, ...), custom_call_target="tpu_custom_call" | custom-call | flops 3000000000 | bytes 10000000 | tf_op jit(solution)/shard_map/pallas_call | solution.py:88
  80.5 2.7 %constant_dynamic-slice_fusion = (bf16[1,128,1024]{2,1,0:T(8,128)(2,1)}, bf16[1,128,1024]{2,1,0:T(8,128)(2,1)}, bf16[1,128,1024]{2,1,0:T(8,128)(2,1)}, bf16[1,12...) fusion(bf16[8,128,1024]{2,1,0:T(8,128)(2,1)} %constant_dynamic-, ...), kind=kLoop, calls=%fused_computation.106 | loop fusion | bytes 3670044 | tf_op jit(solution)/shard_map/jit(dynamic_index_in_dim)/dynamic_slice | solution.py:305
  83.2 3.1 %collective-permute-start.10 = (bf16[1,128,1024]{2,1,0:T(8,128)(2,1)}, bf16[1,128,1024]{2,1,0:T(8,128)(2,1)}, u32[]{:S(2)}, u32[]{:S(2)}) collective-permute-start(bf16[1,128,1024]{2,1,0:T(8,128)(2,1)} %get-tuple-element.37), channel_id=1, source_target_pairs={{0,4},{4,8},{8,12},{12,16},{16,20},{20,24},{24,28},{28,0},{1,5},{5... | collective-permute-start | bytes 786440 | tf_op jit(solution)/shard_map/ppermute | solution.py:309
  87.9 2.5 collective-permute-start.12
  91.3 4.9 %fusion.102 = (bf16[2,2,1,128,2048]{4,3,2,1,0:T(8,128)(2,1)}, bf16[2,2,1,128,2048]{4,3,2,1,0:T(8,128)(2,1)}) fusion(bf16[2,2,2,128,2048]{4,3,2,1,0:T(8,128)(2,1)} %bitcast.99), kind=kLoop, calls=%fused_computation.212 | loop fusion | bytes 8388608 | tf_op jit(solution)/shard_map/slice | solution.py:253
  96.1 2.5 constant_dynamic-slice_fusion.9
  100.9 2.6 add_convert_fusion.3
  105.0 2.6 add_convert_fusion.1
  107.6 2.2 gather_fusion.2
  110.9 20.5 %all_gather.21 = bf16[8,16,2048]{2,1,0:T(8,128)(2,1)S(1)} all-gather(bf16[8,16,512]{2,1,0:T(8,128)(2,1)S(1)} %get-tuple-element.39), channel_id=1, replica_groups=mesh['req'=8,'mlp'=4] {'mlp'}, dimensions={2}, use_global_device_ids=true | all-gather | bytes 655360 | tf_op jit(solution)/shard_map/all_gather | solution.py:193
  132.8 5.4 %all-gather = bf16[16,16,128]{2,1,0:T(8,128)(2,1)S(1)} all-gather(bf16[4,16,128]{2,1,0:T(8,128)(2,1)S(1)} %gather_fusion.4), channel_id=2, replica_groups=mesh['req'=8,'mlp'=4] {'mlp'}, dimensions={0}, use_global_device_ids=true | all-gather | bytes 81920 | tf_op jit(solution)/shard_map/all_gather | solution.py:237
  140.3 2.6 convert_reduce_fusion.2
  144.2 21.3 %all-gather.1 = bf16[16,16,128]{2,1,0:T(8,128)(2,1)S(1)} all-gather(bf16[4,16,128]{2,1,0:T(8,128)(2,1)S(1)} %gather_fusion.7), channel_id=3, replica_groups=mesh['req'=8,'mlp'=4] {'mlp'}, dimensions={0}, use_global_device_ids=true | all-gather | bytes 81920 | tf_op jit(solution)/shard_map/all_gather | solution.py:237
  166.6 2.6 convert_reduce_fusion.1
  169.6 2.0 fusion.32
  175.9 2.7 %collective-permute-start.14 = (bf16[1,128,1024]{2,1,0:T(8,128)(2,1)S(1)}, bf16[1,128,1024]{2,1,0:T(8,128)(2,1)S(1)}, u32[]{:S(2)}, u32[]{:S(2)}) collective-permute-start(bf16[1,128,1024]{2,1,0:T(8,128)(2,1)S(1)} %copy-done.23), channel_id=1, source_target_pairs={{0,20},{4,24},{8,28},{12,0},{16,4},{20,8},{24,12},{28,16},{1,21},{... | collective-permute-start | bytes 786440 | tf_op jit(solution)/shard_map/ppermute | solution.py:309
  178.6 1.7 constant_dynamic-update-slice_fusion.8
  181.5 1.7 constant_dynamic-update-slice_fusion.7
  185.4 16.6 %convolution_convert_fusion = bf16[512,2048]{1,0:T(8,128)(2,1)} fusion(bf16[2048,2048]{1,0:T(8,128)(2,1)} %param.27, bf16[2048,2048]{1,0:T(8,128)(2,1)} %param.26, bf16[256,2048]{1,0:T(8,128)(2,1)} %collective-permute-done.7, bf16[256,2048]{1,0:T(8,128)(2,1)} %get-tuple-element.41), kind=kOutput, calls=%fused_computation.33 | convolution fusion | flops 8604614656 | bytes 20971520 | tf_op jit(solution)/shard_map/dot_general | solution.py:267
  202.0 2.3 slice.89
  204.8 16.9 %convolution_convert_fusion.1 = bf16[512,2048]{1,0:T(8,128)(2,1)} fusion(bf16[2048,2048]{1,0:T(8,128)(2,1)} %param.27, bf16[2048,2048]{1,0:T(8,128)(2,1)} %param.26, bf16[256,2048]{1,0:T(8,128)(2,1)} %collective-permute-done.2, bf16[256,2048]{1,0:T(8,128)(2,1)} %get-tuple-element.40), kind=kOutput, calls=%fused_computation.34 | convolution fusion | flops 8604614656 | bytes 20971520 | tf_op jit(solution)/shard_map/dot_general | solution.py:267
  223.2 1.7 constant_dynamic-update-slice_fusion.5
  226.4 1.8 add_convert_fusion
  229.1 1.6 collective-permute-start.9
  232.7 1.7 constant_dynamic-update-slice_fusion.2.refs_1_
  234.4 6.7 %shard_map.178 = bf16[8,128,1024]{2,1,0:T(8,128)(2,1)} custom-call(s32[8]{0:T(128)} %copy-done.24, s32[8]{0:T(128)} %fusion.89.source, s32[8]{0:T(128)} %convert_element_type.213.came, bf16[8,128,1024]{2,1,0:T(8,128)(2,1)} %constant_dynamic-update-slice_fusion.refs_0_, bf16[7,128,1024]{2,1,0:T(8,128)(2,1)} %constant_dynamic-update-slice_fusion.2.refs_1_), custom_call_target="tpu_custom_call" | custom-call | tf_op jit(solution)/shard_map/pallas_call | solution.py:129
  241.1 2.9 %collective-permute-done.9 = bf16[128,2048]{1,0:T(8,128)(2,1)} collective-permute-done((bf16[128,2048]{1,0:T(8,128)(2,1)S(1)}, bf16[128,2048]{1,0:T(8,128)(2,1)}, u32[]{:S(2)}, u32[]{:S(2)}) %collective-permute-start.9) | collective-permute-done | bytes 524320 | tf_op jit(solution)/shard_map/ppermute | solution.py:282
  245.5 9.4 %collective-permute-done.4 = bf16[128,2048]{1,0:T(8,128)(2,1)} collective-permute-done((bf16[128,2048]{1,0:T(8,128)(2,1)S(1)}, bf16[128,2048]{1,0:T(8,128)(2,1)}, u32[]{:S(2)}, u32[]{:S(2)}) %collective-permute-start.4) | collective-permute-done | bytes 524320 | tf_op jit(solution)/shard_map/ppermute | solution.py:282
  (160 shorter events, 45.2 us)
Async XLA Ops:
  7.2 100.4 %all-gather.4.cloned.1.call-start = ((), (), s32[]{:S(2)}) async-start(), calls=%async_computation | async-start | bytes 2359296 | tf_op jit(solution)/shard_map/all_gather | solution.py:188
  16.1 10.6 %copy-start.2 = (bf16[12,128,1024]{2,1,0:T(8,128)(2,1)S(1)}, bf16[12,128,1024]{2,1,0:T(8,128)(2,1)}, u32[]{:S(2)}) copy-start(bf16[12,128,1024]{2,1,0:T(8,128)(2,1)} %refs_3_.3) | copy-start | bytes 9437188
  16.1 10.6 %copy-start.3 = (bf16[512,2048]{1,0:T(8,128)(2,1)S(1)}, bf16[512,2048]{1,0:T(8,128)(2,1)}, u32[]{:S(2)}) copy-start(bf16[512,2048]{1,0:T(8,128)(2,1)} %refs_4_.3) | copy-start | bytes 6291460
  16.1 10.6 %copy-start.12 = (s32[8]{0:T(128)S(1)}, s32[8]{0:T(128)}, u32[]{:S(2)}) copy-start(s32[8]{0:T(128)} %lens.3) | copy-start | bytes 100
  36.1 10.9 %copy-start.4 = (bf16[512,2048]{1,0:T(8,128)(2,1)}, bf16[512,2048]{1,0:T(8,128)(2,1)S(1)}, u32[]{:S(2)}) copy-start(bf16[512,2048]{1,0:T(8,128)(2,1)S(1)} %get-tuple-element.10) | copy-start | bytes 6291460
  36.1 10.9 %copy-start.10 = (bf16[512,512]{1,0:T(8,128)(2,1)}, bf16[512,512]{1,0:T(8,128)(2,1)S(1)}, u32[]{:S(2)}) copy-start(bf16[512,512]{1,0:T(8,128)(2,1)S(1)} %get-tuple-element.11) | copy-start | bytes 1572868
  37.2 62.4 %collective-permute-start = (bf16[256,2048]{1,0:T(8,128)(2,1)}, bf16[256,2048]{1,0:T(8,128)(2,1)}, u32[]{:S(2)}, u32[]{:S(2)}) collective-permute-start(bf16[256,2048]{1,0:T(8,128)(2,1)} %slice.50), channel_id=1, source_target_pairs={{0,1},{1,0},{2,3},{3,2},{4,5},{5,4},{6,7},{7,6},{8,9},{9,8},{10,11... | collective-permute-start | bytes 3145736 | tf_op jit(solution)/shard_map/ppermute | solution.py:248
  49.9 53.6 %collective-permute-start.5 = (bf16[256,2048]{1,0:T(8,128)(2,1)}, bf16[256,2048]{1,0:T(8,128)(2,1)}, u32[]{:S(2)}, u32[]{:S(2)}) collective-permute-start(bf16[256,2048]{1,0:T(8,128)(2,1)} %slice.59), channel_id=1, source_target_pairs={{0,1},{1,0},{2,3},{3,2},{4,5},{5,4},{6,7},{7,6},{8,9},{9,8},{10,11... | collective-permute-start | bytes 3145736 | tf_op jit(solution)/shard_map/ppermute | solution.py:248
  60.1 16.2 %copy-start.24 = (s32[8]{0:T(128)}, s32[8]{0:T(128)S(1)}, u32[]{:S(2)}) copy-start(s32[8]{0:T(128)S(1)} %get-tuple-element.14.place) | copy-start | bytes 100
  76.3 14.3 %copy-start.13 = (s32[64]{0:T(128)S(1)}, s32[64]{0:T(128)}, u32[]{:S(2)}) copy-start(s32[64]{0:T(128)} %param.24) | copy-start | bytes 772
  83.2 92.6 %collective-permute-start.10 = (bf16[1,128,1024]{2,1,0:T(8,128)(2,1)}, bf16[1,128,1024]{2,1,0:T(8,128)(2,1)}, u32[]{:S(2)}, u32[]{:S(2)}) collective-permute-start(bf16[1,128,1024]{2,1,0:T(8,128)(2,1)} %get-tuple-element.37), channel_id=1, source_target_pairs={{0,4},{4,8},{8,12},{12,16},{16,20},{20,24},{24,28},{28,0},{1,5},{5... | collective-permute-start | bytes 786440 | tf_op jit(solution)/shard_map/ppermute | solution.py:309
  86.4 93.9 %collective-permute-start.11 = (bf16[1,128,1024]{2,1,0:T(8,128)(2,1)}, bf16[1,128,1024]{2,1,0:T(8,128)(2,1)}, u32[]{:S(2)}, u32[]{:S(2)}) collective-permute-start(bf16[1,128,1024]{2,1,0:T(8,128)(2,1)} %get-tuple-element.36), channel_id=1, source_target_pairs={{0,8},{4,12},{8,16},{12,20},{16,24},{20,28},{24,0},{28,4},{1,9},{5... | collective-permute-start | bytes 786440 | tf_op jit(solution)/shard_map/ppermute | solution.py:309
  87.9 95.2 %collective-permute-start.12 = (bf16[1,128,1024]{2,1,0:T(8,128)(2,1)}, bf16[1,128,1024]{2,1,0:T(8,128)(2,1)S(1)}, u32[]{:S(2)}, u32[]{:S(2)}) collective-permute-start(bf16[1,128,1024]{2,1,0:T(8,128)(2,1)} %get-tuple-element.35), channel_id=1, source_target_pairs={{0,12},{4,16},{8,20},{12,24},{16,28},{20,0},{24,4},{28,8},{1,13},{... | collective-permute-start | bytes 786440 | tf_op jit(solution)/shard_map/ppermute | solution.py:309
  96.1 4.7 %copy-start.5 = (bf16[512,2048]{1,0:T(8,128)(2,1)S(1)}, bf16[512,2048]{1,0:T(8,128)(2,1)}, u32[]{:S(2)}) copy-start(bf16[512,2048]{1,0:T(8,128)(2,1)} %copy-done.4) | copy-start | bytes 6291460
  99.7 123.4 %collective-permute-start.13 = (bf16[1,128,1024]{2,1,0:T(8,128)(2,1)}, bf16[1,128,1024]{2,1,0:T(8,128)(2,1)}, u32[]{:S(2)}, u32[]{:S(2)}) collective-permute-start(bf16[1,128,1024]{2,1,0:T(8,128)(2,1)} %get-tuple-element.34), channel_id=1, source_target_pairs={{0,16},{4,20},{8,24},{12,28},{16,0},{20,4},{24,8},{28,12},{1,17},{... | collective-permute-start | bytes 786440 | tf_op jit(solution)/shard_map/ppermute | solution.py:309
  103.5 28.5 %copy-start.11 = (bf16[512,512]{1,0:T(8,128)(2,1)S(1)}, bf16[512,512]{1,0:T(8,128)(2,1)}, u32[]{:S(2)}) copy-start(bf16[512,512]{1,0:T(8,128)(2,1)} %copy-done.10) | copy-start | bytes 1572868
  103.5 35.2 %collective-permute-start.1 = (bf16[256,2048]{1,0:T(8,128)(2,1)}, bf16[256,2048]{1,0:T(8,128)(2,1)}, u32[]{:S(2)}, u32[]{:S(2)}) collective-permute-start(bf16[256,2048]{1,0:T(8,128)(2,1)} %add_convert_fusion.3), channel_id=1, source_target_pairs={{0,2},{1,3},{2,0},{3,1},{4,6},{5,7},{6,4},{7,5},{8,10},{9,11},{10,... | collective-permute-start | bytes 3145736 | tf_op jit(solution)/shard_map/ppermute | solution.py:181
  138.7 27.8 %collective-permute-start.6 = (bf16[256,2048]{1,0:T(8,128)(2,1)}, bf16[256,2048]{1,0:T(8,128)(2,1)}, u32[]{:S(2)}, u32[]{:S(2)}) collective-permute-start(bf16[256,2048]{1,0:T(8,128)(2,1)} %add_convert_fusion.1), channel_id=1, source_target_pairs={{0,2},{1,3},{2,0},{3,1},{4,6},{5,7},{6,4},{7,5},{8,10},{9,11},{10,... | collective-permute-start | bytes 3145736 | tf_op jit(solution)/shard_map/ppermute | solution.py:181
  169.6 6.3 %copy-start.23 = (bf16[1,128,1024]{2,1,0:T(8,128)(2,1)S(1)}, bf16[1,128,1024]{2,1,0:T(8,128)(2,1)}, u32[]{:S(2)}) copy-start(bf16[1,128,1024]{2,1,0:T(8,128)(2,1)} %get-tuple-element.33) | copy-start | bytes 786436
  169.6 10.7 %copy-start.22 = (bf16[1,128,1024]{2,1,0:T(8,128)(2,1)S(1)}, bf16[1,128,1024]{2,1,0:T(8,128)(2,1)}, u32[]{:S(2)}) copy-start(bf16[1,128,1024]{2,1,0:T(8,128)(2,1)} %get-tuple-element.32) | copy-start | bytes 786436
  171.6 13.8 %collective-permute-start.7 = (bf16[256,2048]{1,0:T(8,128)(2,1)}, bf16[256,2048]{1,0:T(8,128)(2,1)}, u32[]{:S(2)}, u32[]{:S(2)}) collective-permute-start(bf16[256,2048]{1,0:T(8,128)(2,1)} %get-tuple-element.41), channel_id=1, source_target_pairs={{0,1},{1,0},{2,3},{3,2},{4,5},{5,4},{6,7},{7,6},{8,9},{9,8},{10,11... | collective-permute-start | bytes 3145736 | tf_op jit(solution)/shard_map/ppermute | solution.py:259
  175.9 49.0 %collective-permute-start.14 = (bf16[1,128,1024]{2,1,0:T(8,128)(2,1)S(1)}, bf16[1,128,1024]{2,1,0:T(8,128)(2,1)S(1)}, u32[]{:S(2)}, u32[]{:S(2)}) collective-permute-start(bf16[1,128,1024]{2,1,0:T(8,128)(2,1)S(1)} %copy-done.23), channel_id=1, source_target_pairs={{0,20},{4,24},{8,28},{12,0},{16,4},{20,8},{24,12},{28,16},{1,21},{... | collective-permute-start | bytes 786440 | tf_op jit(solution)/shard_map/ppermute | solution.py:309
  180.3 45.3 %collective-permute-start.15 = (bf16[1,128,1024]{2,1,0:T(8,128)(2,1)S(1)}, bf16[1,128,1024]{2,1,0:T(8,128)(2,1)S(1)}, u32[]{:S(2)}, u32[]{:S(2)}) collective-permute-start(bf16[1,128,1024]{2,1,0:T(8,128)(2,1)S(1)} %copy-done.22), channel_id=1, source_target_pairs={{0,24},{4,28},{8,0},{12,4},{16,8},{20,12},{24,16},{28,20},{1,25},{... | collective-permute-start | bytes 786440 | tf_op jit(solution)/shard_map/ppermute | solution.py:309
  183.2 49.6 %collective-permute-start.16 = (bf16[1,128,1024]{2,1,0:T(8,128)(2,1)}, bf16[1,128,1024]{2,1,0:T(8,128)(2,1)}, u32[]{:S(2)}, u32[]{:S(2)}) collective-permute-start(bf16[1,128,1024]{2,1,0:T(8,128)(2,1)} %get-tuple-element.31), channel_id=1, source_target_pairs={{0,28},{4,0},{8,4},{12,8},{16,12},{20,16},{24,20},{28,24},{1,29},{... | collective-permute-start | bytes 786440 | tf_op jit(solution)/shard_map/ppermute | solution.py:309
  185.4 18.9 %collective-permute-start.2 = (bf16[256,2048]{1,0:T(8,128)(2,1)}, bf16[256,2048]{1,0:T(8,128)(2,1)}, u32[]{:S(2)}, u32[]{:S(2)}) collective-permute-start(bf16[256,2048]{1,0:T(8,128)(2,1)} %get-tuple-element.40), channel_id=1, source_target_pairs={{0,1},{1,0},{2,3},{3,2},{4,5},{5,4},{6,7},{7,6},{8,9},{9,8},{10,11... | collective-permute-start | bytes 3145736 | tf_op jit(solution)/shard_map/ppermute | solution.py:259
  204.3 22.1 %collective-permute-start.8 = (bf16[256,2048]{1,0:T(8,128)(2,1)}, bf16[256,2048]{1,0:T(8,128)(2,1)}, u32[]{:S(2)}, u32[]{:S(2)}) collective-permute-start(bf16[256,2048]{1,0:T(8,128)(2,1)} %slice.89), channel_id=1, source_target_pairs={{0,1},{1,0},{2,3},{3,2},{4,5},{5,4},{6,7},{7,6},{8,9},{9,8},{10,11... | collective-permute-start | bytes 3145736 | tf_op jit(solution)/shard_map/ppermute | solution.py:270
  221.6 4.7 %copy-start.20 = (bf16[512,2048]{1,0:T(8,128)(2,1)S(1)}, bf16[512,2048]{1,0:T(8,128)(2,1)}, u32[]{:S(2)}) copy-start(bf16[512,2048]{1,0:T(8,128)(2,1)} %convolution_convert_fusion) | copy-start | bytes 6291460
  223.1 7.6 %collective-permute-start.3 = (bf16[256,2048]{1,0:T(8,128)(2,1)S(1)}, bf16[256,2048]{1,0:T(8,128)(2,1)S(1)}, u32[]{:S(2)}, u32[]{:S(2)}) collective-permute-start(bf16[256,2048]{1,0:T(8,128)(2,1)S(1)} %slice.86), channel_id=1, source_target_pairs={{0,1},{1,0},{2,3},{3,2},{4,5},{5,4},{6,7},{7,6},{8,9},{9,8},{10,11... | collective-permute-start | bytes 3145736 | tf_op jit(solution)/shard_map/ppermute | solution.py:270
  226.3 4.4 %copy-start.19 = (bf16[512,2048]{1,0:T(8,128)(2,1)S(1)}, bf16[512,2048]{1,0:T(8,128)(2,1)}, u32[]{:S(2)}) copy-start(bf16[512,2048]{1,0:T(8,128)(2,1)} %convolution_convert_fusion.1) | copy-start | bytes 6291460
  229.1 14.9 %collective-permute-start.9 = (bf16[128,2048]{1,0:T(8,128)(2,1)S(1)}, bf16[128,2048]{1,0:T(8,128)(2,1)}, u32[]{:S(2)}, u32[]{:S(2)}) collective-permute-start(bf16[128,2048]{1,0:T(8,128)(2,1)S(1)} %dynamic-slice_bitcast_fusion), channel_id=1, source_target_pairs={{0,2},{1,3},{2,0},{3,1},{4,6},{5,7},{6,4},{7,5},{8,10},{9,11},{10,... | collective-permute-start | bytes 1572872 | tf_op jit(solution)/shard_map/ppermute | solution.py:282
  232.2 22.7 %collective-permute-start.4 = (bf16[128,2048]{1,0:T(8,128)(2,1)S(1)}, bf16[128,2048]{1,0:T(8,128)(2,1)}, u32[]{:S(2)}, u32[]{:S(2)}) collective-permute-start(bf16[128,2048]{1,0:T(8,128)(2,1)S(1)} %dynamic-slice_bitcast_fusion.1), channel_id=1, source_target_pairs={{0,2},{1,3},{2,0},{3,1},{4,6},{5,7},{6,4},{7,5},{8,10},{9,11},{10,... | collective-permute-start | bytes 1572872 | tf_op jit(solution)/shard_map/ppermute | solution.py:282
  241.1 13.8 %copy-start.18 = (bf16[256,2048]{1,0:T(8,128)(2,1)S(1)}, bf16[256,2048]{1,0:T(8,128)(2,1)}, u32[]{:S(2)}) copy-start(bf16[256,2048]{1,0:T(8,128)(2,1)} %copy-done.17) | copy-start | bytes 3145732
  (15 other events, 27.4 us)
Sparse Core Ops, SparseCore 0:
  10.1 52.1 all-gather.3

commit v2 on v1

--- a/solution.py
+++ b/solution.py
@@ -11,6 +11,7 @@
 HEADS = 16
 HD = 128
 ADAPTERS = 64
+ACTIVE = 16
 CORES = 2
 
 
@@ -111,34 +112,36 @@
     )(order, pages, lens, slopes, joined, *([pool] * n_pages), dense_weight)
 
 
-def merge_body(source, came, fresh, arrived, out):
-    here = came[pl.program_id(0)]
+def merge_body(distance, fresh, *refs):
+    here = distance[pl.program_id(0)]
+    out = refs[-1]
 
     @pl.when(here == 0)
     def _():
         out[...] = fresh[...]
 
-    @pl.when(here != 0)
-    def _():
-        out[...] = arrived[...]
-
-
-def merge(fresh, place, arrived, source, came):
-    requests = came.shape[0]
+    for k in range(1, len(refs)):
+
+        @pl.when(here == k)
+        def _(k=k):
+            out[...] = refs[k - 1][...]
+
+
+def merge(fresh, place, arrived, distance):
+    requests = distance.shape[0]
     block = (1,) + fresh.shape[1:]
     return pl.pallas_call(
-        lambda place, source, came, *refs: merge_body(source, came, *refs),
+        lambda place, distance, *refs: merge_body(distance, *refs),
         grid_spec=pltpu.PrefetchScalarGridSpec(
-            num_scalar_prefetch=3,
+            num_scalar_prefetch=2,
             grid=(requests,),
-            in_specs=[
-                pl.BlockSpec(block, lambda i, p, s, c: (p[i], 0, 0)),
-                pl.BlockSpec(block, lambda i, p, s, c: (s[i], 0, 0)),
-            ],
-            out_specs=pl.BlockSpec(block, lambda i, p, s, c: (i, 0, 0)),
+            in_specs=[pl.BlockSpec(block, lambda i, p, d: (p[i], 0, 0))]
+            + [pl.BlockSpec(block, lambda i, p, d: (0, 0, 0))] * len(arrived),
+            out_specs=pl.BlockSpec(block, lambda i, p, d: (i, 0, 0)),
         ),
         out_shape=jax.ShapeDtypeStruct(fresh.shape, fresh.dtype),
-    )(place, source, came, fresh, arrived)
+        compiler_params=pltpu.CompilerParams(vmem_limit_bytes=20 * 1024 * 1024),
+    )(place, distance, fresh, *arrived)
 
 
 def shards(
@@ -185,12 +188,32 @@
     table_rows = adapter_rows[local_ids]
     cols = adapter_down.shape[2]
     own_up = lax.dynamic_slice_in_dim(adapter_up, mlp_index * cols, cols, axis=2)
-    tables = lax.all_gather(
-        jnp.concatenate([adapter_down, own_up], axis=2), "req", axis=0, tiled=True
+    used = jnp.any(
+        adapter_rows[adapter_ids][:, None] == jnp.arange(ADAPTERS, dtype=jnp.int32)[None, :], axis=0
     )
-    chosen = tables[table_rows]
+    rank = jnp.cumsum(used.astype(jnp.int32)) - 1
+    held = adapter_down.shape[0]
+    held_rank = jnp.where(
+        lax.dynamic_slice_in_dim(used, req_index * held, held),
+        lax.dynamic_slice_in_dim(rank, req_index * held, held),
+        -1,
+    )
+    put = jnp.arange(ACTIVE, dtype=jnp.int32)[:, None] == held_rank[None, :]
+    spread = jnp.einsum(
+        "ah,hkd->akd",
+        put.astype(jnp.bfloat16),
+        jnp.concatenate([adapter_down, own_up], axis=2),
+        preferred_element_type=jnp.float32,
+    ).astype(jnp.bfloat16)
+    tables = lax.psum(spread, "req")
+    chosen = tables[rank[table_rows]]
     chosen_down = chosen[:, :, :cols]
-    chosen_up = lax.all_gather(chosen[:, :, cols:], "mlp", axis=2, tiled=True)
+    up_parts = [chosen[:, :, cols:]]
+    for k in range(1, mlp_count):
+        pairs = [(m, (m + k) % mlp_count) for m in range(mlp_count)]
+        up_parts.append(lax.ppermute(up_parts[0], "mlp", pairs))
+    up_parts = jnp.stack(up_parts, axis=0)
+    up_parts = up_parts[(mlp_index - jnp.arange(mlp_count, dtype=jnp.int32)) % mlp_count]
 
     normed = layer_norm(tokens, first_gain)
     joined = jnp.dot(normed, joined_weight, preferred_element_type=jnp.float32).astype(jnp.bfloat16)
@@ -221,29 +244,34 @@
         (order[None, :] == jnp.arange(requests, dtype=jnp.int32)[:, None]).astype(jnp.int32), axis=1
     ).astype(jnp.int32)
 
+    every = jnp.concatenate([f[0].reshape(mlp_count, slot, local_heads * HD) for f in firsts])
+    low_part = lax.dot_general(
+        chosen_down[order], every, (((2,), (2,)), ((0,), (0,))), preferred_element_type=jnp.float32
+    ).astype(jnp.bfloat16)[place]
+    low_all = low_part.astype(jnp.float32)
+    for k in range(1, mlp_count):
+        pairs = [(m, (m + k) % mlp_count) for m in range(mlp_count)]
+        low_all = low_all + lax.ppermute(low_part, "mlp", pairs).astype(jnp.float32)
+    low_all = low_all.astype(jnp.bfloat16)
+
     outs = []
     for c in range(own_requests):
         attended, dense_part = firsts[c]
-        low_part = lax.dot_general(
-            chosen_down[orders[c]],
-            attended.reshape(mlp_count, slot, local_heads * HD),
-            (((2,), (2,)), ((0,), (0,))),
-            preferred_element_type=jnp.float32,
-        ).astype(jnp.bfloat16)
-        in_order = jnp.arange(mlp_count, dtype=jnp.int32) // CORES
-        swap = in_order + (
-            (jnp.arange(mlp_count, dtype=jnp.int32) % CORES + core_index) % CORES
-        ) * rows
-        every_low = lax.all_gather(low_part[swap], "mlp", axis=0, tiled=False)
-        low_all = jnp.sum(every_low.astype(jnp.float32), axis=0).astype(jnp.bfloat16)
         mine = orders[c][:rows]
-        low = low_all.reshape(rows, CORES, low_all.shape[1], slot)
+        low = low_all.reshape(rows, CORES, own_requests, low_all.shape[1], slot)[:, :, c]
         low = lax.dynamic_index_in_dim(low, core_index, axis=1, keepdims=False)
-        delta = lax.dot_general(
-            low,
-            chosen_up[mine],
-            (((1,), (1,)), ((0,), (0,))),
-            preferred_element_type=jnp.float32,
+        own_ups = up_parts[:, mine]
+        delta = jnp.concatenate(
+            [
+                lax.dot_general(
+                    low,
+                    own_ups[m],
+                    (((1,), (1,)), ((0,), (0,))),
+                    preferred_element_type=jnp.float32,
+                )
+                for m in range(mlp_count)
+            ],
+            axis=2,
         ).reshape(half, width)
         other = lax.ppermute(dense_part[half:], "mlp", core_pairs)
         pair_sum = (dense_part[:half].astype(jnp.float32) + other.astype(jnp.float32)).astype(
@@ -307,10 +335,8 @@
         )
         pairs = [(r, (r + k) % req_count) for r in range(req_count)]
         arrived.append(lax.ppermute(send, "req", pairs))
-    arrived = jnp.concatenate(arrived, axis=0)
-    source = jnp.where(came > 0, (req_index - owner - 1) % req_count, 0).astype(jnp.int32)
-    source = jnp.clip(source, 0, req_count - 2)
-    page_out = merge(fresh, place, arrived, source, came)
+    distance = jnp.where(came > 0, (req_index - owner) % req_count, 0).astype(jnp.int32)
+    page_out = merge(fresh, place, arrived, distance)
     return (layer_out, page_out)
 
 

time: 265 us -> 301 us (1.14)
  the two profiles are of different devices: /device:TPU:0 before, /device:TPU:24 now
where the time goes in v2:
time: 301 us; the launch traced here: 300 us
  waiting for transfers between devices  96.8 us (32%)
  matrix products  51.4 us (17%)
  between operations  41.1 us (14%)
  local copies, waits for them, and re-layouts  39.7 us (13%)
  other arithmetic  27.8 us (9%)
  Pallas kernels  23.5 us (8%)
  starting transfers between devices  19.8 us (7%)
    ppermute x2, waiting for transfers between devices, across_rows(): out.append(lax.ppermute(values, 'mlp', pairs))  42.8 us
    dot_general x2, matrix products, shards(): jnp.dot(expanded, down_weight, preferred_element_type=jnp.float32)  33.4 us
    ppermute x7, waiting for transfers between devices, shards(): arrived.append(lax.ppermute(send, 'req', pairs))  23 us
    psum x1, waiting for transfers between devices, shards(): tables = lax.psum(spread, 'req')  19.6 us
    pallas_call x2, Pallas kernels, attend(): pl.pallas_call(functools.partial(attend_body, local_heads, n_pages), grid...  18.8 us
    dot_general x1, matrix products, shards(): jnp.dot(normed, joined_weight, preferred_element_type=jnp.float32)  10.6 us
    ppermute x7, starting transfers between devices, shards(): arrived.append(lax.ppermute(send, 'req', pairs))  9.91 us
    ppermute x2, waiting for transfers between devices, shards(): feed = feed + lax.ppermute(send, 'mlp', pairs).astype(jnp.float32)  6.03 us
  transfers between devices with their start and end apart: 24, of which 9 were waited for; matrix products, arithmetic and copies ran while one was open for 35% of the time, Pallas kernels for 8%

profile of v2, /device:TPU:24, one launch (start us, length us, event | category | flops | bytes accessed | tf_op | source)
XLA Modules:
  0.0 300.2 jit_solution(7230539424973411870)
XLA Ops:
  13.3 3.0 convert_reduce_fusion
  18.6 10.6 %fusion.20.joined = bf16[1024,1536]{1,0:T(8,128)(2,1)S(1)} fusion(bf16[2048,1536]{1,0:T(8,128)(2,1)} %param.19, bf16[1024,2048]{1,0:T(8,128)(2,1)} %param.17, f32[2048]{0:T(1024)S(1)} %copy-done.31, f32[1024]{0:T(1024)S(1)} %add_rsqrt_fusion, f32[1024]{0:T(1024)S(1)} %broadcast_multiply_fusion), kind=kOutput, calls=%fused_computation.33 | convolution fusion | flops 6454509568 | bytes 13647872 | tf_op jit(solution)/shard_map/dot_general | solution.py:219
  29.3 9.5 %shard_map.177 = (bf16[512,512]{1,0:T(8,128)(2,1)S(1)}, bf16[4,128,1024]{2,1,0:T(8,128)(2,1)S(1)}, bf16[512,2048]{1,0:T(8,128)(2,1)S(1)}) custom-call(s32[4]{0:T(128)S(1)} %get-tuple-element.58.order, s32[8,4]{1,0:T(8,128)S(1)} %gather_fusion, s32[8]{0:T(128)S(1)} %copy-done.7, f32[4]{0:T(128)S(1)} %multiply_exponential_fusion.slopes, ...), custom_call_target="tpu_custom_call" | custom-call | flops 3000000000 | bytes 10000000 | tf_op jit(solution)/shard_map/pallas_call | solution.py:89
  40.8 9.4 %shard_map.176 = (bf16[512,512]{1,0:T(8,128)(2,1)S(1)}, bf16[4,128,1024]{2,1,0:T(8,128)(2,1)S(1)}, bf16[512,2048]{1,0:T(8,128)(2,1)S(1)}) custom-call(s32[4]{0:T(128)S(1)} %mul.177.order, s32[8,4]{1,0:T(8,128)S(1)} %gather_fusion, s32[8]{0:T(128)S(1)} %copy-done.7, f32[4]{0:T(128)S(1)} %multiply_exponential_fusion.slopes, ...), custom_call_target="tpu_custom_call" | custom-call | flops 3000000000 | bytes 10000000 | tf_op jit(solution)/shard_map/pallas_call | solution.py:89
  56.8 4.8 %fusion.121 = (bf16[2,2,1,128,2048]{4,3,2,1,0:T(8,128)(2,1)}, bf16[2,2,1,128,2048]{4,3,2,1,0:T(8,128)(2,1)}) fusion(bf16[2,2,2,128,2048]{4,3,2,1,0:T(8,128)(2,1)} %bitcast.147), kind=kLoop, calls=%fused_computation.245 | loop fusion | bytes 8388608 | tf_op jit(solution)/shard_map/slice | solution.py:281
  61.7 2.6 constant_dynamic-slice_fusion.8
  65.3 19.6 %all-reduce.2.cloned.1.call-done = bf16[16,16,1024]{2,0,1:T(8,128)(2,1)} async-done(((bf16[16,16,1024]{2,0,1:T(8,128)(2,1)}), bf16[16,16,1024]{2,0,1:T(8,128)(2,1)}) %all-reduce.2.cloned.1.call-update) | async-done | bytes 524304 | tf_op jit(solution)/shard_map/psum | solution.py:208
  84.9 2.1 copy.45
  87.0 1.6 gather_fusion.4
  90.2 1.6 convolution_convert_fusion.3
  92.5 1.6 collective-permute-start.3
  96.5 1.5 collective-permute-start.6
  98.8 2.3 collective-permute-done.5
  101.1 1.9 collective-permute-done.6
  104.7 2.4 gather_fusion.7
  107.1 1.6 gather_fusion.9
  111.9 1.6 gather_fusion.8
  114.1 1.7 pad_maximum_fusion.1
  116.2 1.6 add_convert_fusion.1
  119.2 1.6 add_convert_fusion.3
  122.3 21.6 %collective-permute-done.12 = bf16[256,2048]{1,0:T(8,128)(2,1)S(1)} collective-permute-done((bf16[256,2048]{1,0:T(8,128)(2,1)S(1)}, bf16[256,2048]{1,0:T(8,128)(2,1)S(1)}, u32[]{:S(2)}, u32[]{:S(2)}) %collective-permute-start.12) | collective-permute-done | bytes 1048608 | tf_op jit(solution)/shard_map/ppermute | solution.py:184
  145.0 21.3 %collective-permute-done.1 = bf16[256,2048]{1,0:T(8,128)(2,1)S(1)} collective-permute-done((bf16[256,2048]{1,0:T(8,128)(2,1)S(1)}, bf16[256,2048]{1,0:T(8,128)(2,1)S(1)}, u32[]{:S(2)}, u32[]{:S(2)}) %collective-permute-start.1) | collective-permute-done | bytes 1048608 | tf_op jit(solution)/shard_map/ppermute | solution.py:184
  167.5 2.0 fusion.32
  201.0 1.6 collective-permute-start.17
  202.6 2.1 collective-permute-start.18
  206.2 16.6 %convolution_convert_fusion.1 = bf16[512,2048]{1,0:T(8,128)(2,1)} fusion(bf16[2048,2048]{1,0:T(8,128)(2,1)} %param.27, bf16[2048,2048]{1,0:T(8,128)(2,1)} %param.26, bf16[256,2048]{1,0:T(8,128)(2,1)} %collective-permute-done.8, bf16[256,2048]{1,0:T(8,128)(2,1)} %get-tuple-element.45), kind=kOutput, calls=%fused_computation.35 | convolution fusion | flops 8604614656 | bytes 20971520 | tf_op jit(solution)/shard_map/dot_general | solution.py:295
  222.8 2.3 slice.133
  225.6 16.8 %convolution_convert_fusion = bf16[512,2048]{1,0:T(8,128)(2,1)} fusion(bf16[2048,2048]{1,0:T(8,128)(2,1)} %param.27, bf16[2048,2048]{1,0:T(8,128)(2,1)} %param.26, bf16[256,2048]{1,0:T(8,128)(2,1)} %collective-permute-done.13, bf16[256,2048]{1,0:T(8,128)(2,1)} %get-tuple-element.46), kind=kOutput, calls=%fused_computation.34 | convolution fusion | flops 8604614656 | bytes 20971520 | tf_op jit(solution)/shard_map/dot_general | solution.py:295
  249.6 1.6 collective-permute-start.20
  254.3 23.0 %collective-permute-done.19.refs_4_ = bf16[1,128,1024]{2,1,0:T(8,128)(2,1)S(1)} collective-permute-done((bf16[1,128,1024]{2,1,0:T(8,128)(2,1)}, bf16[1,128,1024]{2,1,0:T(8,128)(2,1)S(1)}, u32[]{:S(2)}, u32[]{:S(2)}) %collective-permute-start.19) | collective-permute-done | bytes 262176 | tf_op jit(solution)/shard_map/ppermute | solution.py:337
  278.6 4.7 %shard_map.178 = bf16[8,128,1024]{2,1,0:T(8,128)(2,1)} custom-call(s32[8]{0:T(128)S(1)} %get-tuple-element.13.place, s32[8]{0:T(128)S(1)} %compare_select_fusion.23.distance, bf16[8,128,1024]{2,1,0:T(8,128)(2,1)S(1)} %constant_dynamic-update-slice_fusion.refs_0_, bf16[1,128,1024]{2,1,0:T(8,128)(2,1)S(1)} %collective-permute-done.16.refs_1_, ...), custom_call_target="tpu_custom_call" | custom-call | tf_op jit(solution)/shard_map/pallas_call | solution.py:133
  284.8 6.0 %collective-permute-done.15 = bf16[128,2048]{1,0:T(8,128)(2,1)} collective-permute-done((bf16[128,2048]{1,0:T(8,128)(2,1)}, bf16[128,2048]{1,0:T(8,128)(2,1)}, u32[]{:S(2)}, u32[]{:S(2)}) %collective-permute-start.15) | collective-permute-done | bytes 524320 | tf_op jit(solution)/shard_map/ppermute | solution.py:310
  (195 shorter events, 57.1 us)
Async XLA Ops:
  7.2 77.7 %all-reduce.2.cloned.1.call-start = ((), (), s32[]{:S(2)}) async-start(), calls=%async_computation | async-start | bytes 1048576 | tf_op jit(solution)/shard_map/psum | solution.py:208
  18.6 10.7 %copy-start.2 = (bf16[12,128,1024]{2,1,0:T(8,128)(2,1)S(1)}, bf16[12,128,1024]{2,1,0:T(8,128)(2,1)}, u32[]{:S(2)}) copy-start(bf16[12,128,1024]{2,1,0:T(8,128)(2,1)} %refs_3_.3) | copy-start | bytes 9437188
  18.6 10.7 %copy-start.3 = (bf16[512,2048]{1,0:T(8,128)(2,1)S(1)}, bf16[512,2048]{1,0:T(8,128)(2,1)}, u32[]{:S(2)}) copy-start(bf16[512,2048]{1,0:T(8,128)(2,1)} %refs_4_.3) | copy-start | bytes 6291460
  40.8 75.3 %collective-permute-start.11 = (bf16[256,2048]{1,0:T(8,128)(2,1)}, bf16[256,2048]{1,0:T(8,128)(2,1)}, u32[]{:S(2)}, u32[]{:S(2)}) collective-permute-start(bf16[256,2048]{1,0:T(8,128)(2,1)} %slice.94), channel_id=1, source_target_pairs={{0,1},{1,0},{2,3},{3,2},{4,5},{5,4},{6,7},{7,6},{8,9},{9,8},{10,11... | collective-permute-start | bytes 3145736 | tf_op jit(solution)/shard_map/ppermute | solution.py:276
  53.0 66.2 %collective-permute-start = (bf16[256,2048]{1,0:T(8,128)(2,1)}, bf16[256,2048]{1,0:T(8,128)(2,1)}, u32[]{:S(2)}, u32[]{:S(2)}) collective-permute-start(bf16[256,2048]{1,0:T(8,128)(2,1)} %slice.80), channel_id=1, source_target_pairs={{0,1},{1,0},{2,3},{3,2},{4,5},{5,4},{6,7},{7,6},{8,9},{9,8},{10,11... | collective-permute-start | bytes 3145736 | tf_op jit(solution)/shard_map/ppermute | solution.py:276
  89.4 14.4 %copy-start.26 = (bf16[1,8,16,512]{3,2,1,0:T(8,128)(2,1)S(1)}, bf16[1,8,16,512]{3,2,1,0:T(8,128)(2,1)}, u32[]{:S(2)}) copy-start(bf16[1,8,16,512]{3,2,1,0:T(8,128)(2,1)} %get-tuple-element.39) | copy-start | bytes 393220
  92.5 3.6 %collective-permute-start.2 = (bf16[8,16,128]{2,1,0:T(8,128)(2,1)S(1)}, bf16[8,16,128]{2,1,0:T(8,128)(2,1)S(1)}, u32[]{:S(2)}, u32[]{:S(2)}) collective-permute-start(bf16[8,16,128]{2,1,0:T(8,128)(2,1)S(1)} %gather_fusion.6), channel_id=1, source_target_pairs={{0,1},{1,2},{2,3},{3,0},{4,5},{5,6},{6,7},{7,4},{8,9},{9,10},{10,1... | collective-permute-start | bytes 98312 | tf_op jit(solution)/shard_map/ppermute | solution.py:254
  92.5 4.0 %collective-permute-start.3 = (bf16[8,16,128]{2,1,0:T(8,128)(2,1)S(1)}, bf16[8,16,128]{2,1,0:T(8,128)(2,1)S(1)}, u32[]{:S(2)}, u32[]{:S(2)}) collective-permute-start(bf16[8,16,128]{2,1,0:T(8,128)(2,1)S(1)} %gather_fusion.6), channel_id=1, source_target_pairs={{0,2},{1,3},{2,0},{3,1},{4,6},{5,7},{6,4},{7,5},{8,10},{9,11},{10,... | collective-permute-start | bytes 98312 | tf_op jit(solution)/shard_map/ppermute | solution.py:254
  94.1 4.0 %collective-permute-start.4 = (bf16[8,16,128]{2,1,0:T(8,128)(2,1)S(1)}, bf16[8,16,128]{2,1,0:T(8,128)(2,1)S(1)}, u32[]{:S(2)}, u32[]{:S(2)}) collective-permute-start(bf16[8,16,128]{2,1,0:T(8,128)(2,1)S(1)} %gather_fusion.6), channel_id=1, source_target_pairs={{0,3},{1,0},{2,1},{3,2},{4,7},{5,4},{6,5},{7,6},{8,11},{9,8},{10,9... | collective-permute-start | bytes 98312 | tf_op jit(solution)/shard_map/ppermute | solution.py:254
  96.1 5.0 %collective-permute-start.5 = (bf16[8,16,512]{2,1,0:T(8,128)(2,1)}, bf16[8,16,512]{2,1,0:T(8,128)(2,1)S(1)}, u32[]{:S(2)}, u32[]{:S(2)}) collective-permute-start(bf16[8,16,512]{2,1,0:T(8,128)(2,1)} %get-tuple-element.40), channel_id=1, source_target_pairs={{0,1},{1,2},{2,3},{3,0},{4,5},{5,6},{6,7},{7,4},{8,9},{9,10},{10,1... | collective-permute-start | bytes 393224 | tf_op jit(solution)/shard_map/ppermute | solution.py:214
  96.5 6.6 %collective-permute-start.6 = (bf16[8,16,512]{2,1,0:T(8,128)(2,1)}, bf16[8,16,512]{2,1,0:T(8,128)(2,1)S(1)}, u32[]{:S(2)}, u32[]{:S(2)}) collective-permute-start(bf16[8,16,512]{2,1,0:T(8,128)(2,1)} %get-tuple-element.40), channel_id=1, source_target_pairs={{0,2},{1,3},{2,0},{3,1},{4,6},{5,7},{6,4},{7,5},{8,10},{9,11},{10,... | collective-permute-start | bytes 393224 | tf_op jit(solution)/shard_map/ppermute | solution.py:214
  98.0 5.7 %collective-permute-start.7 = (bf16[8,16,512]{2,1,0:T(8,128)(2,1)}, bf16[8,16,512]{2,1,0:T(8,128)(2,1)S(1)}, u32[]{:S(2)}, u32[]{:S(2)}) collective-permute-start(bf16[8,16,512]{2,1,0:T(8,128)(2,1)} %get-tuple-element.40), channel_id=1, source_target_pairs={{0,3},{1,0},{2,1},{3,2},{4,7},{5,4},{6,5},{7,6},{8,11},{9,8},{10,9... | collective-permute-start | bytes 393224 | tf_op jit(solution)/shard_map/ppermute | solution.py:214
  117.7 26.1 %collective-permute-start.12 = (bf16[256,2048]{1,0:T(8,128)(2,1)S(1)}, bf16[256,2048]{1,0:T(8,128)(2,1)S(1)}, u32[]{:S(2)}, u32[]{:S(2)}) collective-permute-start(bf16[256,2048]{1,0:T(8,128)(2,1)S(1)} %add_convert_fusion.1), channel_id=1, source_target_pairs={{0,2},{1,3},{2,0},{3,1},{4,6},{5,7},{6,4},{7,5},{8,10},{9,11},{10,... | collective-permute-start | bytes 3145736 | tf_op jit(solution)/shard_map/ppermute | solution.py:184
  120.9 23.0 %copy-start.22 = (bf16[2,1,1,128,2048]{4,3,2,1,0:T(8,128)(2,1)S(1)}, bf16[2,1,1,128,2048]{4,3,2,1,0:T(8,128)(2,1)}, u32[]{:S(2)}) copy-start(bf16[2,1,1,128,2048]{4,3,2,1,0:T(8,128)(2,1)} %constant_dynamic-slice_fusion.8) | copy-start | bytes 3145732
  120.9 45.4 %collective-permute-start.1 = (bf16[256,2048]{1,0:T(8,128)(2,1)S(1)}, bf16[256,2048]{1,0:T(8,128)(2,1)S(1)}, u32[]{:S(2)}, u32[]{:S(2)}) collective-permute-start(bf16[256,2048]{1,0:T(8,128)(2,1)S(1)} %add_convert_fusion.3), channel_id=1, source_target_pairs={{0,2},{1,3},{2,0},{3,1},{4,6},{5,7},{6,4},{7,5},{8,10},{9,11},{10,... | collective-permute-start | bytes 3145736 | tf_op jit(solution)/shard_map/ppermute | solution.py:184
  122.3 44.0 %copy-start.21 = (bf16[2,1,1,128,2048]{4,3,2,1,0:T(8,128)(2,1)S(1)}, bf16[2,1,1,128,2048]{4,3,2,1,0:T(8,128)(2,1)}, u32[]{:S(2)}) copy-start(bf16[2,1,1,128,2048]{4,3,2,1,0:T(8,128)(2,1)} %constant_dynamic-slice_fusion.12) | copy-start | bytes 3145732
  144.6 22.9 %copy-start.12 = (bf16[256,2048]{1,0:T(8,128)(2,1)}, bf16[256,2048]{1,0:T(8,128)(2,1)S(1)}, u32[]{:S(2)}) copy-start(bf16[256,2048]{1,0:T(8,128)(2,1)S(1)} %get-tuple-element.28) | copy-start | bytes 3145732
  145.0 22.5 %copy-start.27 = (f32[2048]{0:T(1024)S(1)}, f32[2048]{0:T(1024)}, u32[]{:S(2)}) copy-start(f32[2048]{0:T(1024)} %param.25) | copy-start | bytes 24580
  169.5 36.7 %collective-permute-start.8 = (bf16[256,2048]{1,0:T(8,128)(2,1)}, bf16[256,2048]{1,0:T(8,128)(2,1)}, u32[]{:S(2)}, u32[]{:S(2)}) collective-permute-start(bf16[256,2048]{1,0:T(8,128)(2,1)} %get-tuple-element.45), channel_id=1, source_target_pairs={{0,1},{1,0},{2,3},{3,2},{4,5},{5,4},{6,7},{7,6},{8,9},{9,8},{10,11... | collective-permute-start | bytes 3145736 | tf_op jit(solution)/shard_map/ppermute | solution.py:287
  200.1 49.4 %collective-permute-start.16 = (bf16[1,128,1024]{2,1,0:T(8,128)(2,1)S(1)}, bf16[1,128,1024]{2,1,0:T(8,128)(2,1)S(1)}, u32[]{:S(2)}, u32[]{:S(2)}) collective-permute-start(bf16[1,128,1024]{2,1,0:T(8,128)(2,1)S(1)} %get-tuple-element.37), channel_id=1, source_target_pairs={{0,4},{4,8},{8,12},{12,16},{16,20},{20,24},{24,28},{28,0},{1,5},{5... | collective-permute-start | bytes 786440 | tf_op jit(solution)/shard_map/ppermute | solution.py:337
  201.0 50.1 %collective-permute-start.17 = (bf16[1,128,1024]{2,1,0:T(8,128)(2,1)}, bf16[1,128,1024]{2,1,0:T(8,128)(2,1)S(1)}, u32[]{:S(2)}, u32[]{:S(2)}) collective-permute-start(bf16[1,128,1024]{2,1,0:T(8,128)(2,1)} %get-tuple-element.36), channel_id=1, source_target_pairs={{0,8},{4,12},{8,16},{12,20},{16,24},{20,28},{24,0},{28,4},{1,9},{5... | collective-permute-start | bytes 786440 | tf_op jit(solution)/shard_map/ppermute | solution.py:337
  202.6 49.5 %collective-permute-start.18 = (bf16[1,128,1024]{2,1,0:T(8,128)(2,1)}, bf16[1,128,1024]{2,1,0:T(8,128)(2,1)S(1)}, u32[]{:S(2)}, u32[]{:S(2)}) collective-permute-start(bf16[1,128,1024]{2,1,0:T(8,128)(2,1)} %get-tuple-element.35), channel_id=1, source_target_pairs={{0,12},{4,16},{8,20},{12,24},{16,28},{20,0},{24,4},{28,8},{1,13},{... | collective-permute-start | bytes 786440 | tf_op jit(solution)/shard_map/ppermute | solution.py:337
  206.2 19.4 %collective-permute-start.13 = (bf16[256,2048]{1,0:T(8,128)(2,1)}, bf16[256,2048]{1,0:T(8,128)(2,1)}, u32[]{:S(2)}, u32[]{:S(2)}) collective-permute-start(bf16[256,2048]{1,0:T(8,128)(2,1)} %get-tuple-element.46), channel_id=1, source_target_pairs={{0,1},{1,0},{2,3},{3,2},{4,5},{5,4},{6,7},{7,6},{8,9},{9,8},{10,11... | collective-permute-start | bytes 3145736 | tf_op jit(solution)/shard_map/ppermute | solution.py:287
  225.1 19.5 %collective-permute-start.9 = (bf16[256,2048]{1,0:T(8,128)(2,1)}, bf16[256,2048]{1,0:T(8,128)(2,1)}, u32[]{:S(2)}, u32[]{:S(2)}) collective-permute-start(bf16[256,2048]{1,0:T(8,128)(2,1)} %slice.133), channel_id=1, source_target_pairs={{0,1},{1,0},{2,3},{3,2},{4,5},{5,4},{6,7},{7,6},{8,9},{9,8},{10,11... | collective-permute-start | bytes 3145736 | tf_op jit(solution)/shard_map/ppermute | solution.py:298
  243.9 4.7 %collective-permute-start.14 = (bf16[256,2048]{1,0:T(8,128)(2,1)S(1)}, bf16[256,2048]{1,0:T(8,128)(2,1)S(1)}, u32[]{:S(2)}, u32[]{:S(2)}) collective-permute-start(bf16[256,2048]{1,0:T(8,128)(2,1)S(1)} %slice.141), channel_id=1, source_target_pairs={{0,1},{1,0},{2,3},{3,2},{4,5},{5,4},{6,7},{7,6},{8,9},{9,8},{10,11... | collective-permute-start | bytes 3145736 | tf_op jit(solution)/shard_map/ppermute | solution.py:298
  244.6 32.7 %collective-permute-start.19 = (bf16[1,128,1024]{2,1,0:T(8,128)(2,1)}, bf16[1,128,1024]{2,1,0:T(8,128)(2,1)S(1)}, u32[]{:S(2)}, u32[]{:S(2)}) collective-permute-start(bf16[1,128,1024]{2,1,0:T(8,128)(2,1)} %get-tuple-element.34), channel_id=1, source_target_pairs={{0,16},{4,20},{8,24},{12,28},{16,0},{20,4},{24,8},{28,12},{1,17},{... | collective-permute-start | bytes 786440 | tf_op jit(solution)/shard_map/ppermute | solution.py:337
  248.5 34.8 %collective-permute-start.10 = (bf16[128,2048]{1,0:T(8,128)(2,1)}, bf16[128,2048]{1,0:T(8,128)(2,1)}, u32[]{:S(2)}, u32[]{:S(2)}) collective-permute-start(bf16[128,2048]{1,0:T(8,128)(2,1)} %dynamic-slice_bitcast_fusion.1), channel_id=1, source_target_pairs={{0,2},{1,3},{2,0},{3,1},{4,6},{5,7},{6,4},{7,5},{8,10},{9,11},{10,... | collective-permute-start | bytes 1572872 | tf_op jit(solution)/shard_map/ppermute | solution.py:310
  249.5 27.8 %copy-start.19 = (bf16[256,2048]{1,0:T(8,128)(2,1)}, bf16[256,2048]{1,0:T(8,128)(2,1)S(1)}, u32[]{:S(2)}) copy-start(bf16[256,2048]{1,0:T(8,128)(2,1)S(1)} %add_convert_fusion) | copy-start | bytes 3145732
  249.6 29.1 %collective-permute-start.20 = (bf16[1,128,1024]{2,1,0:T(8,128)(2,1)}, bf16[1,128,1024]{2,1,0:T(8,128)(2,1)S(1)}, u32[]{:S(2)}, u32[]{:S(2)}) collective-permute-start(bf16[1,128,1024]{2,1,0:T(8,128)(2,1)} %get-tuple-element.33), channel_id=1, source_target_pairs={{0,20},{4,24},{8,28},{12,0},{16,4},{20,8},{24,12},{28,16},{1,21},{... | collective-permute-start | bytes 786440 | tf_op jit(solution)/shard_map/ppermute | solution.py:337
  251.1 27.5 %collective-permute-start.21 = (bf16[1,128,1024]{2,1,0:T(8,128)(2,1)}, bf16[1,128,1024]{2,1,0:T(8,128)(2,1)}, u32[]{:S(2)}, u32[]{:S(2)}) collective-permute-start(bf16[1,128,1024]{2,1,0:T(8,128)(2,1)} %get-tuple-element.32), channel_id=1, source_target_pairs={{0,24},{4,28},{8,0},{12,4},{16,8},{20,12},{24,16},{28,20},{1,25},{... | collective-permute-start | bytes 786440 | tf_op jit(solution)/shard_map/ppermute | solution.py:337
  252.1 26.5 %collective-permute-start.22 = (bf16[1,128,1024]{2,1,0:T(8,128)(2,1)}, bf16[1,128,1024]{2,1,0:T(8,128)(2,1)}, u32[]{:S(2)}, u32[]{:S(2)}) collective-permute-start(bf16[1,128,1024]{2,1,0:T(8,128)(2,1)} %get-tuple-element.31), channel_id=1, source_target_pairs={{0,28},{4,0},{8,4},{12,8},{16,12},{20,16},{24,20},{28,24},{1,29},{... | collective-permute-start | bytes 786440 | tf_op jit(solution)/shard_map/ppermute | solution.py:337
  277.3 13.6 %collective-permute-start.15 = (bf16[128,2048]{1,0:T(8,128)(2,1)}, bf16[128,2048]{1,0:T(8,128)(2,1)}, u32[]{:S(2)}, u32[]{:S(2)}) collective-permute-start(bf16[128,2048]{1,0:T(8,128)(2,1)} %dynamic-slice_bitcast_fusion), channel_id=1, source_target_pairs={{0,2},{1,3},{2,0},{3,1},{4,6},{5,7},{6,4},{7,5},{8,10},{9,11},{10,... | collective-permute-start | bytes 1572872 | tf_op jit(solution)/shard_map/ppermute | solution.py:310
  (25 other events, 91.2 us)
Sparse Core Ops, SparseCore 0:
  12.5 72.3 all-reduce.1

commit v3 on v2

--- a/solution.py
+++ b/solution.py
@@ -11,7 +11,6 @@
 HEADS = 16
 HD = 128
 ADAPTERS = 64
-ACTIVE = 16
 CORES = 2
 
 
@@ -112,36 +111,34 @@
     )(order, pages, lens, slopes, joined, *([pool] * n_pages), dense_weight)
 
 
-def merge_body(distance, fresh, *refs):
-    here = distance[pl.program_id(0)]
-    out = refs[-1]
+def merge_body(came, fresh, arrived, out):
+    here = came[pl.program_id(0)]
 
     @pl.when(here == 0)
     def _():
         out[...] = fresh[...]
 
-    for k in range(1, len(refs)):
-
-        @pl.when(here == k)
-        def _(k=k):
-            out[...] = refs[k - 1][...]
-
-
-def merge(fresh, place, arrived, distance):
-    requests = distance.shape[0]
+    @pl.when(here != 0)
+    def _():
+        out[...] = arrived[...]
+
+
+def merge(fresh, place, arrived, owner, came):
+    requests = came.shape[0]
     block = (1,) + fresh.shape[1:]
     return pl.pallas_call(
-        lambda place, distance, *refs: merge_body(distance, *refs),
+        lambda place, owner, came, *refs: merge_body(came, *refs),
         grid_spec=pltpu.PrefetchScalarGridSpec(
-            num_scalar_prefetch=2,
+            num_scalar_prefetch=3,
             grid=(requests,),
-            in_specs=[pl.BlockSpec(block, lambda i, p, d: (p[i], 0, 0))]
-            + [pl.BlockSpec(block, lambda i, p, d: (0, 0, 0))] * len(arrived),
-            out_specs=pl.BlockSpec(block, lambda i, p, d: (i, 0, 0)),
+            in_specs=[
+                pl.BlockSpec(block, lambda i, p, o, c: (p[i], 0, 0)),
+                pl.BlockSpec(block, lambda i, p, o, c: (o[i], 0, 0)),
+            ],
+            out_specs=pl.BlockSpec(block, lambda i, p, o, c: (i, 0, 0)),
         ),
         out_shape=jax.ShapeDtypeStruct(fresh.shape, fresh.dtype),
-        compiler_params=pltpu.CompilerParams(vmem_limit_bytes=20 * 1024 * 1024),
-    )(place, distance, fresh, *arrived)
+    )(place, owner, came, fresh, arrived)
 
 
 def shards(
@@ -188,32 +185,9 @@
     table_rows = adapter_rows[local_ids]
     cols = adapter_down.shape[2]
     own_up = lax.dynamic_slice_in_dim(adapter_up, mlp_index * cols, cols, axis=2)
-    used = jnp.any(
-        adapter_rows[adapter_ids][:, None] == jnp.arange(ADAPTERS, dtype=jnp.int32)[None, :], axis=0
-    )
-    rank = jnp.cumsum(used.astype(jnp.int32)) - 1
-    held = adapter_down.shape[0]
-    held_rank = jnp.where(
-        lax.dynamic_slice_in_dim(used, req_index * held, held),
-        lax.dynamic_slice_in_dim(rank, req_index * held, held),
-        -1,
-    )
-    put = jnp.arange(ACTIVE, dtype=jnp.int32)[:, None] == held_rank[None, :]
-    spread = jnp.einsum(
-        "ah,hkd->akd",
-        put.astype(jnp.bfloat16),
-        jnp.concatenate([adapter_down, own_up], axis=2),
-        preferred_element_type=jnp.float32,
-    ).astype(jnp.bfloat16)
-    tables = lax.psum(spread, "req")
-    chosen = tables[rank[table_rows]]
-    chosen_down = chosen[:, :, :cols]
-    up_parts = [chosen[:, :, cols:]]
-    for k in range(1, mlp_count):
-        pairs = [(m, (m + k) % mlp_count) for m in range(mlp_count)]
-        up_parts.append(lax.ppermute(up_parts[0], "mlp", pairs))
-    up_parts = jnp.stack(up_parts, axis=0)
-    up_parts = up_parts[(mlp_index - jnp.arange(mlp_count, dtype=jnp.int32)) % mlp_count]
+    own_table = jnp.concatenate([adapter_down, own_up], axis=2)
+    own_table, tokens = lax.optimization_barrier((own_table, tokens))
+    tables = lax.all_gather(own_table, "req", axis=0, tiled=True)
 
     normed = layer_norm(tokens, first_gain)
     joined = jnp.dot(normed, joined_weight, preferred_element_type=jnp.float32).astype(jnp.bfloat16)
@@ -244,6 +218,36 @@
         (order[None, :] == jnp.arange(requests, dtype=jnp.int32)[:, None]).astype(jnp.int32), axis=1
     ).astype(jnp.int32)
 
+    moves = migrants.shape[0]
+    my_landing = lax.dynamic_slice_in_dim(landing, req_index * moves, moves)
+    own_slots = req_index * requests + jnp.arange(requests, dtype=jnp.int32)
+    lands_here = landing[None, :] == own_slots[:, None]
+    came = jnp.any(lands_here, axis=1).astype(jnp.int32)
+    owner = jnp.argmax(lands_here.astype(jnp.int32), axis=1).astype(jnp.int32) // moves
+    hit = my_landing[None, :] // requests == jnp.arange(req_count, dtype=jnp.int32)[:, None]
+    leaving = place[jnp.sum(hit.astype(jnp.int32) * migrants[None, :], axis=1)]
+    arrived = lax.all_to_all(fresh[leaving], "req", 0, 0, tiled=True)
+    owner = jnp.where(came > 0, owner, 0).astype(jnp.int32)
+
+    crossed = []
+    for c in range(own_requests):
+        dense_part = firsts[c][1]
+        other = lax.ppermute(dense_part[half:], "mlp", core_pairs)
+        pair_sum = (dense_part[:half].astype(jnp.float32) + other.astype(jnp.float32)).astype(
+            jnp.bfloat16
+        )
+        crossed.append(across_rows(pair_sum))
+    barred = lax.optimization_barrier((tables, crossed[0][-1], crossed[-1][0]))
+    tables = barred[0]
+    chosen = tables[table_rows]
+    chosen_down = chosen[:, :, :cols]
+    up_parts = [chosen[:, :, cols:]]
+    for k in range(1, mlp_count):
+        pairs = [(m, (m + k) % mlp_count) for m in range(mlp_count)]
+        up_parts.append(lax.ppermute(up_parts[0], "mlp", pairs))
+    up_parts = jnp.stack(up_parts, axis=0)
+    up_parts = up_parts[(mlp_index - jnp.arange(mlp_count, dtype=jnp.int32)) % mlp_count]
+
     every = jnp.concatenate([f[0].reshape(mlp_count, slot, local_heads * HD) for f in firsts])
     low_part = lax.dot_general(
         chosen_down[order], every, (((2,), (2,)), ((0,), (0,))), preferred_element_type=jnp.float32
@@ -256,7 +260,6 @@
 
     outs = []
     for c in range(own_requests):
-        attended, dense_part = firsts[c]
         mine = orders[c][:rows]
         low = low_all.reshape(rows, CORES, own_requests, low_all.shape[1], slot)[:, :, c]
         low = lax.dynamic_index_in_dim(low, core_index, axis=1, keepdims=False)
@@ -273,11 +276,7 @@
             ],
             axis=2,
         ).reshape(half, width)
-        other = lax.ppermute(dense_part[half:], "mlp", core_pairs)
-        pair_sum = (dense_part[:half].astype(jnp.float32) + other.astype(jnp.float32)).astype(
-            jnp.bfloat16
-        )
-        dense = sum(part.astype(jnp.float32) for part in across_rows(pair_sum))
+        dense = sum(part.astype(jnp.float32) for part in crossed[c])
         own_tokens = tokens.reshape(rows, CORES, own_requests, slot, width)[:, :, c]
         own_tokens = lax.dynamic_index_in_dim(own_tokens, core_index, axis=1, keepdims=False)
         residual = (
@@ -320,23 +319,7 @@
         )
     layer_out = jnp.concatenate(outs, axis=0)
 
-    moves = migrants.shape[0]
-    my_landing = lax.dynamic_slice_in_dim(landing, req_index * moves, moves)
-    own_slots = req_index * requests + jnp.arange(requests, dtype=jnp.int32)
-    lands_here = landing[None, :] == own_slots[:, None]
-    came = jnp.any(lands_here, axis=1).astype(jnp.int32)
-    owner = jnp.argmax(lands_here.astype(jnp.int32), axis=1).astype(jnp.int32) // moves
-    arrived = []
-    for k in range(1, req_count):
-        to = (req_index + k) % req_count
-        hit = (my_landing // requests == to).astype(jnp.int32)
-        send = lax.dynamic_index_in_dim(
-            fresh, place[jnp.sum(hit * migrants)], axis=0, keepdims=True
-        )
-        pairs = [(r, (r + k) % req_count) for r in range(req_count)]
-        arrived.append(lax.ppermute(send, "req", pairs))
-    distance = jnp.where(came > 0, (req_index - owner) % req_count, 0).astype(jnp.int32)
-    page_out = merge(fresh, place, arrived, distance)
+    page_out = merge(fresh, place, arrived, owner, came)
     return (layer_out, page_out)
 
 

time: 301 us -> 228 us (0.76)
  the two profiles are of different devices: /device:TPU:24 before, /device:TPU:0 now
where the time goes in v3:
time: 228 us; the launch traced here: 227 us
  waiting for transfers between devices  56.3 us (25%)
  matrix products  47.4 us (21%)
  local copies, waits for them, and re-layouts  36.1 us (16%)
  other arithmetic  30 us (13%)
  Pallas kernels  25.3 us (11%)
  starting transfers between devices  17.5 us (8%)
  between operations  14.7 us (6%)
    dot_general x2, matrix products, shards(): jnp.dot(expanded, down_weight, preferred_element_type=jnp.float32)  33.1 us
    ppermute x3, waiting for transfers between devices, shards(): up_parts.append(lax.ppermute(up_parts[0], 'mlp', pairs))  27.9 us
    pallas_call x2, Pallas kernels, attend(): pl.pallas_call(functools.partial(attend_body, local_heads, n_pages), grid...  18.6 us
    ppermute x2, waiting for transfers between devices, across_rows(): out.append(lax.ppermute(values, 'mlp', pairs))  17.4 us
    ppermute x2, waiting for transfers between devices, shards(): feed = feed + lax.ppermute(send, 'mlp', pairs).astype(jnp.float32)  10.8 us
    dot_general x1, matrix products, shards(): jnp.dot(normed, joined_weight, preferred_element_type=jnp.float32)  10.6 us
    unnamed x77, local copies, waits for them, and re-layouts  8.51 us
    reduce_sum x3, other arithmetic, layer_norm(): mean = jnp.mean(values, axis=-1, keepdims=True)  7.4 us
  transfers between devices with their start and end apart: 18, of which 5 were waited for; matrix products, arithmetic and copies ran while one was open for 40% of the time, Pallas kernels for 11%

profile of v3, /device:TPU:0, one launch (start us, length us, event | category | flops | bytes accessed | tf_op | source)
XLA Modules:
  0.0 227.3 jit_solution(12725049823075022663)
XLA Ops:
  8.2 1.6 pad_maximum_fusion.4
  10.8 3.0 %convert_reduce_fusion = f32[1024]{0:T(1024)S(1)} fusion(bf16[1024,2048]{1,0:T(8,128)(2,1)} %param.17), kind=kLoop, calls=%fused_computation.11 | loop fusion | flops 4193280 | bytes 4198400 | tf_op jit(solution)/shard_map/reduce_sum | solution.py:22
  16.1 10.6 %fusion.20.joined = bf16[1024,1536]{1,0:T(8,128)(2,1)S(1)} fusion(bf16[2048,1536]{1,0:T(8,128)(2,1)} %param.19, bf16[1024,2048]{1,0:T(8,128)(2,1)} %param.17, f32[2048]{0:T(1024)S(1)} %copy-done.36, f32[1024]{0:T(1024)S(1)} %add_rsqrt_fusion, f32[1024]{0:T(1024)S(1)} %broadcast_multiply_fusion), kind=kOutput, calls=%fused_computation.33 | convolution fusion | flops 6454509568 | bytes 13647872 | tf_op jit(solution)/shard_map/dot_general | solution.py:193
  26.7 9.3 %shard_map.176 = (bf16[512,512]{1,0:T(8,128)(2,1)S(1)}, bf16[4,128,1024]{2,1,0:T(8,128)(2,1)S(1)}, bf16[512,2048]{1,0:T(8,128)(2,1)S(1)}) custom-call(s32[4]{0:T(128)S(1)} %mul.163.order, s32[8,4]{1,0:T(8,128)S(1)} %gather_fusion, s32[8]{0:T(128)S(1)} %copy-done.8, f32[4]{0:T(128)S(1)} %multiply_exponential_fusion.slopes, ...), custom_call_target="tpu_custom_call" | custom-call | flops 3000000000 | bytes 10000000 | tf_op jit(solution)/shard_map/pallas_call | solution.py:88
  37.6 9.3 %shard_map.177 = (bf16[512,512]{1,0:T(8,128)(2,1)S(1)}, bf16[4,128,1024]{2,1,0:T(8,128)(2,1)S(1)}, bf16[512,2048]{1,0:T(8,128)(2,1)S(1)}) custom-call(s32[4]{0:T(128)S(1)} %get-tuple-element.42.order, s32[8,4]{1,0:T(8,128)S(1)} %gather_fusion, s32[8]{0:T(128)S(1)} %copy-done.8, f32[4]{0:T(128)S(1)} %multiply_exponential_fusion.slopes, ...), custom_call_target="tpu_custom_call" | custom-call | flops 3000000000 | bytes 10000000 | tf_op jit(solution)/shard_map/pallas_call | solution.py:88
  51.1 5.0 %fusion.120 = (bf16[2,2,1,128,2048]{4,3,2,1,0:T(8,128)(2,1)}, bf16[2,2,1,128,2048]{4,3,2,1,0:T(8,128)(2,1)}) fusion(bf16[2,2,2,128,2048]{4,3,2,1,0:T(8,128)(2,1)} %bitcast.139), kind=kLoop, calls=%fused_computation.222 | loop fusion | bytes 8388608 | tf_op jit(solution)/shard_map/slice | solution.py:280
  56.1 2.6 %add_convert_fusion.3 = bf16[256,2048]{1,0:T(8,128)(2,1)} fusion(bf16[256,2048]{1,0:T(8,128)(2,1)} %collective-permute-done, bf16[512,2048]{1,0:T(8,128)(2,1)S(1)} %copy-done.5), kind=kLoop, calls=%fused_computation.77 | loop fusion | flops 2097152 | bytes 3145728 | tf_op jit(solution)/shard_map/convert_element_type | solution.py:236
  58.7 3.1 %collective-permute-start.1 = (bf16[256,2048]{1,0:T(8,128)(2,1)}, bf16[256,2048]{1,0:T(8,128)(2,1)}, u32[]{:S(2)}, u32[]{:S(2)}) collective-permute-start(bf16[256,2048]{1,0:T(8,128)(2,1)} %add_convert_fusion.3), channel_id=1, source_target_pairs={{0,2},{1,3},{2,0},{3,1},{4,6},{5,7},{6,4},{7,5},{8,10},{9,11},{10,... | collective-permute-start | bytes 3145736 | tf_op jit(solution)/shard_map/ppermute | solution.py:181
  61.8 2.5 %constant_dynamic-slice_fusion.1 = bf16[2,1,1,128,2048]{4,3,2,1,0:T(8,128)(2,1)} fusion(bf16[2,2,1,128,2048]{4,3,2,1,0:T(8,128)(2,1)} %get-tuple-element.28, s32[]{:T(128)S(6)} %select_n.187), kind=kLoop, calls=%fused_computation.167 | loop fusion | bytes 2097156 | tf_op jit(solution)/shard_map/jit(dynamic_index_in_dim)/dynamic_slice | solution.py:281
  65.4 2.6 %add_convert_fusion.2 = bf16[256,2048]{1,0:T(8,128)(2,1)} fusion(bf16[256,2048]{1,0:T(8,128)(2,1)} %collective-permute-done.2, bf16[512,2048]{1,0:T(8,128)(2,1)S(1)} %get-tuple-element.16), kind=kLoop, calls=%fused_computation.76 | loop fusion | flops 2097152 | bytes 3145728 | tf_op jit(solution)/shard_map/convert_element_type | solution.py:236
  68.0 17.4 %collective-permute-done.1 = bf16[256,2048]{1,0:T(8,128)(2,1)} collective-permute-done((bf16[256,2048]{1,0:T(8,128)(2,1)}, bf16[256,2048]{1,0:T(8,128)(2,1)}, u32[]{:S(2)}, u32[]{:S(2)}) %collective-permute-start.1) | collective-permute-done | bytes 1048608 | tf_op jit(solution)/shard_map/ppermute | solution.py:181
  85.5 2.2 gather_fusion.2
  88.2 1.6 convolution_convert_fusion.2
  93.7 1.5 collective-permute-start.8
  96.5 23.1 %collective-permute-done.8 = bf16[8,16,512]{2,1,0:T(8,128)(2,1)S(1)} collective-permute-done((bf16[8,16,512]{2,1,0:T(8,128)(2,1)S(1)}, bf16[8,16,512]{2,1,0:T(8,128)(2,1)S(1)}, u32[]{:S(2)}, u32[]{:S(2)}) %collective-permute-start.8) | collective-permute-done | bytes 131104 | tf_op jit(solution)/shard_map/ppermute | solution.py:247
  119.7 4.8 %collective-permute-done.7 = bf16[8,16,512]{2,1,0:T(8,128)(2,1)S(1)} collective-permute-done((bf16[8,16,512]{2,1,0:T(8,128)(2,1)S(1)}, bf16[8,16,512]{2,1,0:T(8,128)(2,1)S(1)}, u32[]{:S(2)}, u32[]{:S(2)}) %collective-permute-start.7) | collective-permute-done | bytes 131104 | tf_op jit(solution)/shard_map/ppermute | solution.py:247
  128.1 2.3 %convert_reduce_fusion.2 = (f32[256]{0:T(256)S(1)}, bf16[256,2048]{1,0:T(8,128)(2,1)S(1)}) fusion(f32[2,128,2048]{2,1,0:T(8,128)S(1)} %pad_maximum_fusion, bf16[256,2048]{1,0:T(8,128)(2,1)} %collective-permute-done.1, bf16[256,2048]{1,0:T(8,128)(2,1)} %add_convert_fusion.3, bf16[2,1,1,128,2048]{4,3,2,1,0:T(8,128)(2,1)S(1)} %copy-done.27), kind=kLoop, calls=%fused_computation.39 | loop fusion | flops 4718336 | bytes 6292480 | tf_op jit(solution)/shard_map/reduce_sum | solution.py:22
  130.5 2.0 gather_fusion.7
  135.5 2.1 convert_reduce_fusion.1
  138.1 2.0 fusion.32
  141.4 2.0 gather_fusion.9
  143.4 5.8 %all-to-all-start = ((bf16[8,128,1024]{2,1,0:T(8,128)(2,1)}), bf16[8,128,1024]{2,1,0:T(8,128)(2,1)S(1)}, u32[]{:S(2)}, u32[]{:S(2)}) async-start(bf16[8,128,1024]{2,1,0:T(8,128)(2,1)} %gather_fusion.9), calls=%async_computation | async-start | bytes 4194304 | tf_op jit(solution)/shard_map/all_to_all | solution.py:229
  150.7 16.6 %convolution_convert_fusion = bf16[512,2048]{1,0:T(8,128)(2,1)} fusion(bf16[2048,2048]{1,0:T(8,128)(2,1)} %param.27, bf16[2048,2048]{1,0:T(8,128)(2,1)} %param.26, bf16[256,2048]{1,0:T(8,128)(2,1)} %collective-permute-done.13, bf16[256,2048]{1,0:T(8,128)(2,1)} %get-tuple-element.36), kind=kOutput, calls=%fused_computation.34 | convolution fusion | flops 8604614656 | bytes 20971520 | tf_op jit(solution)/shard_map/dot_general | solution.py:294
  167.3 2.5 %slice.141 = bf16[256,2048]{1,0:T(8,128)(2,1)} slice(bf16[512,2048]{1,0:T(8,128)(2,1)} %convolution_convert_fusion), slice={[256:512], [0:2048]} | slice | bytes 2097152 | tf_op jit(solution)/shard_map/slice | solution.py:297
  170.3 16.5 %convolution_convert_fusion.1 = bf16[512,2048]{1,0:T(8,128)(2,1)} fusion(bf16[2048,2048]{1,0:T(8,128)(2,1)} %param.27, bf16[2048,2048]{1,0:T(8,128)(2,1)} %param.26, bf16[256,2048]{1,0:T(8,128)(2,1)} %collective-permute-done.9, bf16[256,2048]{1,0:T(8,128)(2,1)S(1)} %copy-done.31), kind=kOutput, calls=%fused_computation.35 | convolution fusion | flops 8604614656 | bytes 20971520 | tf_op jit(solution)/shard_map/dot_general | solution.py:294
  186.8 1.4 slice.133
  189.5 1.8 add_convert_fusion
  199.1 6.7 %shard_map.178 = bf16[8,128,1024]{2,1,0:T(8,128)(2,1)} custom-call(s32[8]{0:T(128)} %copy-done.11, s32[8]{0:T(128)} %compare_select_fusion.14.owner, s32[8]{0:T(128)} %convert_element_type.219.came, bf16[8,128,1024]{2,1,0:T(8,128)(2,1)} %copy-done.14, bf16[8,128,1024]{2,1,0:T(8,128)(2,1)} %copy-done.19), custom_call_target="tpu_custom_call" | custom-call | tf_op jit(solution)/shard_map/pallas_call | solution.py:129
  205.8 1.5 collective-permute-done.15
  207.2 1.5 fusion.60
  208.7 9.4 %collective-permute-done.11 = bf16[128,2048]{1,0:T(8,128)(2,1)} collective-permute-done((bf16[128,2048]{1,0:T(8,128)(2,1)}, bf16[128,2048]{1,0:T(8,128)(2,1)}, u32[]{:S(2)}, u32[]{:S(2)}) %collective-permute-start.11) | collective-permute-done | bytes 524320 | tf_op jit(solution)/shard_map/ppermute | solution.py:309
  218.1 1.4 fusion.63
  (184 shorter events, 37.2 us)
Async XLA Ops:
  7.2 78.3 %all-gather.2.cloned.1.call-start = ((), (), s32[]{:S(2)}) async-start(), calls=%async_computation.1 | async-start | bytes 2359296 | tf_op jit(solution)/shard_map/all_gather | solution.py:190
  16.0 10.6 %copy-start.2 = (bf16[12,128,1024]{2,1,0:T(8,128)(2,1)S(1)}, bf16[12,128,1024]{2,1,0:T(8,128)(2,1)}, u32[]{:S(2)}) copy-start(bf16[12,128,1024]{2,1,0:T(8,128)(2,1)} %refs_3_.3) | copy-start | bytes 9437188
  16.1 10.6 %copy-start.3 = (bf16[512,2048]{1,0:T(8,128)(2,1)S(1)}, bf16[512,2048]{1,0:T(8,128)(2,1)}, u32[]{:S(2)}) copy-start(bf16[512,2048]{1,0:T(8,128)(2,1)} %refs_4_.3) | copy-start | bytes 6291460
  16.1 10.6 %copy-start.8 = (s32[8]{0:T(128)S(1)}, s32[8]{0:T(128)}, u32[]{:S(2)}) copy-start(s32[8]{0:T(128)} %lens.3) | copy-start | bytes 100
  36.0 10.9 %copy-start.4 = (bf16[512,2048]{1,0:T(8,128)(2,1)}, bf16[512,2048]{1,0:T(8,128)(2,1)S(1)}, u32[]{:S(2)}) copy-start(bf16[512,2048]{1,0:T(8,128)(2,1)S(1)} %get-tuple-element.14) | copy-start | bytes 6291460
  36.0 10.9 %copy-start.9 = (bf16[512,512]{1,0:T(8,128)(2,1)}, bf16[512,512]{1,0:T(8,128)(2,1)S(1)}, u32[]{:S(2)}) copy-start(bf16[512,512]{1,0:T(8,128)(2,1)S(1)} %get-tuple-element.18) | copy-start | bytes 1572868
  37.1 19.0 %collective-permute-start = (bf16[256,2048]{1,0:T(8,128)(2,1)}, bf16[256,2048]{1,0:T(8,128)(2,1)}, u32[]{:S(2)}, u32[]{:S(2)}) collective-permute-start(bf16[256,2048]{1,0:T(8,128)(2,1)} %slice.80), channel_id=1, source_target_pairs={{0,1},{1,0},{2,3},{3,2},{4,5},{5,4},{6,7},{7,6},{8,9},{9,8},{10,11... | collective-permute-start | bytes 3145736 | tf_op jit(solution)/shard_map/ppermute | solution.py:235
  49.1 16.4 %collective-permute-start.2 = (bf16[256,2048]{1,0:T(8,128)(2,1)}, bf16[256,2048]{1,0:T(8,128)(2,1)}, u32[]{:S(2)}, u32[]{:S(2)}) collective-permute-start(bf16[256,2048]{1,0:T(8,128)(2,1)} %slice.82), channel_id=1, source_target_pairs={{0,1},{1,0},{2,3},{3,2},{4,5},{5,4},{6,7},{7,6},{8,9},{9,8},{10,11... | collective-permute-start | bytes 3145736 | tf_op jit(solution)/shard_map/ppermute | solution.py:235
  49.9 42.5 %copy-start.11 = (s32[8]{0:T(128)}, s32[8]{0:T(128)S(1)}, u32[]{:S(2)}) copy-start(s32[8]{0:T(128)S(1)} %get-tuple-element.20.place) | copy-start | bytes 100
  51.1 5.0 %copy-start.5 = (bf16[512,2048]{1,0:T(8,128)(2,1)S(1)}, bf16[512,2048]{1,0:T(8,128)(2,1)}, u32[]{:S(2)}) copy-start(bf16[512,2048]{1,0:T(8,128)(2,1)} %copy-done.4) | copy-start | bytes 6291460
  58.7 26.8 %collective-permute-start.1 = (bf16[256,2048]{1,0:T(8,128)(2,1)}, bf16[256,2048]{1,0:T(8,128)(2,1)}, u32[]{:S(2)}, u32[]{:S(2)}) collective-permute-start(bf16[256,2048]{1,0:T(8,128)(2,1)} %add_convert_fusion.3), channel_id=1, source_target_pairs={{0,2},{1,3},{2,0},{3,1},{4,6},{5,7},{6,4},{7,5},{8,10},{9,11},{10,... | collective-permute-start | bytes 3145736 | tf_op jit(solution)/shard_map/ppermute | solution.py:181
  68.0 25.1 %copy-start.21 = (bf16[256,2048]{1,0:T(8,128)(2,1)S(1)}, bf16[256,2048]{1,0:T(8,128)(2,1)}, u32[]{:S(2)}) copy-start(bf16[256,2048]{1,0:T(8,128)(2,1)} %add_convert_fusion.2) | copy-start | bytes 3145732
  90.4 4.8 %collective-permute-start.5 = (bf16[8,16,128]{2,1,0:T(8,128)(2,1)S(1)}, bf16[8,16,128]{2,1,0:T(8,128)(2,1)S(1)}, u32[]{:S(2)}, u32[]{:S(2)}) collective-permute-start(bf16[8,16,128]{2,1,0:T(8,128)(2,1)S(1)} %gather_fusion.4), channel_id=1, source_target_pairs={{0,3},{1,0},{2,1},{3,2},{4,7},{5,4},{6,5},{7,6},{8,11},{9,8},{10,9... | collective-permute-start | bytes 98312 | tf_op jit(solution)/shard_map/ppermute | solution.py:258
  90.9 5.5 %collective-permute-start.4 = (bf16[8,16,128]{2,1,0:T(8,128)(2,1)S(1)}, bf16[8,16,128]{2,1,0:T(8,128)(2,1)S(1)}, u32[]{:S(2)}, u32[]{:S(2)}) collective-permute-start(bf16[8,16,128]{2,1,0:T(8,128)(2,1)S(1)} %gather_fusion.4), channel_id=1, source_target_pairs={{0,2},{1,3},{2,0},{3,1},{4,6},{5,7},{6,4},{7,5},{8,10},{9,11},{10,... | collective-permute-start | bytes 98312 | tf_op jit(solution)/shard_map/ppermute | solution.py:258
  92.3 4.2 %collective-permute-start.3 = (bf16[8,16,128]{2,1,0:T(8,128)(2,1)S(1)}, bf16[8,16,128]{2,1,0:T(8,128)(2,1)S(1)}, u32[]{:S(2)}, u32[]{:S(2)}) collective-permute-start(bf16[8,16,128]{2,1,0:T(8,128)(2,1)S(1)} %gather_fusion.4), channel_id=1, source_target_pairs={{0,1},{1,2},{2,3},{3,0},{4,5},{5,6},{6,7},{7,4},{8,9},{9,10},{10,1... | collective-permute-start | bytes 98312 | tf_op jit(solution)/shard_map/ppermute | solution.py:258
  93.1 41.1 %collective-permute-start.12 = (bf16[256,2048]{1,0:T(8,128)(2,1)S(1)}, bf16[256,2048]{1,0:T(8,128)(2,1)}, u32[]{:S(2)}, u32[]{:S(2)}) collective-permute-start(bf16[256,2048]{1,0:T(8,128)(2,1)S(1)} %copy-done.21), channel_id=1, source_target_pairs={{0,2},{1,3},{2,0},{3,1},{4,6},{5,7},{6,4},{7,5},{8,10},{9,11},{10,... | collective-permute-start | bytes 3145736 | tf_op jit(solution)/shard_map/ppermute | solution.py:181
  93.7 26.0 %collective-permute-start.8 = (bf16[8,16,512]{2,1,0:T(8,128)(2,1)S(1)}, bf16[8,16,512]{2,1,0:T(8,128)(2,1)S(1)}, u32[]{:S(2)}, u32[]{:S(2)}) collective-permute-start(bf16[8,16,512]{2,1,0:T(8,128)(2,1)S(1)} %get-tuple-element.32), channel_id=1, source_target_pairs={{0,3},{1,0},{2,1},{3,2},{4,7},{5,4},{6,5},{7,6},{8,11},{9,8},{10,9... | collective-permute-start | bytes 393224 | tf_op jit(solution)/shard_map/ppermute | solution.py:247
  95.2 29.3 %collective-permute-start.7 = (bf16[8,16,512]{2,1,0:T(8,128)(2,1)S(1)}, bf16[8,16,512]{2,1,0:T(8,128)(2,1)S(1)}, u32[]{:S(2)}, u32[]{:S(2)}) collective-permute-start(bf16[8,16,512]{2,1,0:T(8,128)(2,1)S(1)} %get-tuple-element.32), channel_id=1, source_target_pairs={{0,2},{1,3},{2,0},{3,1},{4,6},{5,7},{6,4},{7,5},{8,10},{9,11},{10,... | collective-permute-start | bytes 393224 | tf_op jit(solution)/shard_map/ppermute | solution.py:247
  96.5 28.0 %collective-permute-start.6 = (bf16[8,16,512]{2,1,0:T(8,128)(2,1)S(1)}, bf16[8,16,512]{2,1,0:T(8,128)(2,1)S(1)}, u32[]{:S(2)}, u32[]{:S(2)}) collective-permute-start(bf16[8,16,512]{2,1,0:T(8,128)(2,1)S(1)} %get-tuple-element.32), channel_id=1, source_target_pairs={{0,1},{1,2},{2,3},{3,0},{4,5},{5,6},{6,7},{7,4},{8,9},{9,10},{10,1... | collective-permute-start | bytes 393224 | tf_op jit(solution)/shard_map/ppermute | solution.py:247
  130.4 7.6 %copy-start.15 = (bf16[256,2048]{1,0:T(8,128)(2,1)}, bf16[256,2048]{1,0:T(8,128)(2,1)S(1)}, u32[]{:S(2)}) copy-start(bf16[256,2048]{1,0:T(8,128)(2,1)S(1)} %get-tuple-element.25) | copy-start | bytes 3145732
  134.2 3.9 %copy-start.33 = (f32[2048]{0:T(1024)S(1)}, f32[2048]{0:T(1024)}, u32[]{:S(2)}) copy-start(f32[2048]{0:T(1024)} %param.25) | copy-start | bytes 24580
  140.1 10.6 %collective-permute-start.13 = (bf16[256,2048]{1,0:T(8,128)(2,1)}, bf16[256,2048]{1,0:T(8,128)(2,1)}, u32[]{:S(2)}, u32[]{:S(2)}) collective-permute-start(bf16[256,2048]{1,0:T(8,128)(2,1)} %get-tuple-element.36), channel_id=1, source_target_pairs={{0,1},{1,0},{2,3},{3,2},{4,5},{5,4},{6,7},{7,6},{8,9},{9,8},{10,11... | collective-permute-start | bytes 3145736 | tf_op jit(solution)/shard_map/ppermute | solution.py:286
  143.4 54.4 %all-to-all-start = ((bf16[8,128,1024]{2,1,0:T(8,128)(2,1)}), bf16[8,128,1024]{2,1,0:T(8,128)(2,1)S(1)}, u32[]{:S(2)}, u32[]{:S(2)}) async-start(bf16[8,128,1024]{2,1,0:T(8,128)(2,1)} %gather_fusion.9), calls=%async_computation | async-start | bytes 4194304 | tf_op jit(solution)/shard_map/all_to_all | solution.py:229
  150.7 19.6 %collective-permute-start.9 = (bf16[256,2048]{1,0:T(8,128)(2,1)}, bf16[256,2048]{1,0:T(8,128)(2,1)}, u32[]{:S(2)}, u32[]{:S(2)}) collective-permute-start(bf16[256,2048]{1,0:T(8,128)(2,1)} %get-tuple-element.35), channel_id=1, source_target_pairs={{0,1},{1,0},{2,3},{3,2},{4,5},{5,4},{6,7},{7,6},{8,9},{9,8},{10,11... | collective-permute-start | bytes 3145736 | tf_op jit(solution)/shard_map/ppermute | solution.py:286
  169.8 19.7 %collective-permute-start.14 = (bf16[256,2048]{1,0:T(8,128)(2,1)}, bf16[256,2048]{1,0:T(8,128)(2,1)}, u32[]{:S(2)}, u32[]{:S(2)}) collective-permute-start(bf16[256,2048]{1,0:T(8,128)(2,1)} %slice.141), channel_id=1, source_target_pairs={{0,1},{1,0},{2,3},{3,2},{4,5},{5,4},{6,7},{7,6},{8,9},{9,8},{10,11... | collective-permute-start | bytes 3145736 | tf_op jit(solution)/shard_map/ppermute | solution.py:297
  188.2 4.8 %collective-permute-start.10 = (bf16[256,2048]{1,0:T(8,128)(2,1)S(1)}, bf16[256,2048]{1,0:T(8,128)(2,1)S(1)}, u32[]{:S(2)}, u32[]{:S(2)}) collective-permute-start(bf16[256,2048]{1,0:T(8,128)(2,1)S(1)} %slice.133), channel_id=1, source_target_pairs={{0,1},{1,0},{2,3},{3,2},{4,5},{5,4},{6,7},{7,6},{8,9},{9,8},{10,11... | collective-permute-start | bytes 3145736 | tf_op jit(solution)/shard_map/ppermute | solution.py:297
  189.5 3.6 %copy-start.28 = (bf16[512,2048]{1,0:T(8,128)(2,1)S(1)}, bf16[512,2048]{1,0:T(8,128)(2,1)}, u32[]{:S(2)}) copy-start(bf16[512,2048]{1,0:T(8,128)(2,1)} %convolution_convert_fusion.1) | copy-start | bytes 6291460
  192.2 15.0 %collective-permute-start.15 = (bf16[128,2048]{1,0:T(8,128)(2,1)}, bf16[128,2048]{1,0:T(8,128)(2,1)}, u32[]{:S(2)}, u32[]{:S(2)}) collective-permute-start(bf16[128,2048]{1,0:T(8,128)(2,1)} %dynamic-slice_bitcast_fusion), channel_id=1, source_target_pairs={{0,2},{1,3},{2,0},{3,1},{4,6},{5,7},{6,4},{7,5},{8,10},{9,11},{10,... | collective-permute-start | bytes 1572872 | tf_op jit(solution)/shard_map/ppermute | solution.py:309
  195.3 22.8 %collective-permute-start.11 = (bf16[128,2048]{1,0:T(8,128)(2,1)}, bf16[128,2048]{1,0:T(8,128)(2,1)}, u32[]{:S(2)}, u32[]{:S(2)}) collective-permute-start(bf16[128,2048]{1,0:T(8,128)(2,1)} %dynamic-slice_bitcast_fusion.1), channel_id=1, source_target_pairs={{0,2},{1,3},{2,0},{3,1},{4,6},{5,7},{6,4},{7,5},{8,10},{9,11},{10,... | collective-permute-start | bytes 1572872 | tf_op jit(solution)/shard_map/ppermute | solution.py:309
  197.7 9.5 %copy-start.18 = (bf16[256,2048]{1,0:T(8,128)(2,1)S(1)}, bf16[256,2048]{1,0:T(8,128)(2,1)}, u32[]{:S(2)}) copy-start(bf16[256,2048]{1,0:T(8,128)(2,1)} %copy-done.17) | copy-start | bytes 3145732
  205.7 12.3 %copy-start.16 = (bf16[256,2048]{1,0:T(8,128)(2,1)S(1)}, bf16[256,2048]{1,0:T(8,128)(2,1)}, u32[]{:S(2)}) copy-start(bf16[256,2048]{1,0:T(8,128)(2,1)} %copy-done.15) | copy-start | bytes 3145732
  205.7 12.3 %copy-start.25 = (bf16[256,2048]{1,0:T(8,128)(2,1)S(1)}, bf16[256,2048]{1,0:T(8,128)(2,1)}, u32[]{:S(2)}) copy-start(bf16[256,2048]{1,0:T(8,128)(2,1)} %copy-done.24) | copy-start | bytes 3145732
  (24 other events, 46.1 us)
Sparse Core Ops, SparseCore 0:
  10.1 52.1 all-gather.1

commit v4 on v3

--- a/solution.py
+++ b/solution.py
@@ -226,7 +226,8 @@
     owner = jnp.argmax(lands_here.astype(jnp.int32), axis=1).astype(jnp.int32) // moves
     hit = my_landing[None, :] // requests == jnp.arange(req_count, dtype=jnp.int32)[:, None]
     leaving = place[jnp.sum(hit.astype(jnp.int32) * migrants[None, :], axis=1)]
-    arrived = lax.all_to_all(fresh[leaving], "req", 0, 0, tiled=True)
+    sending = fresh[leaving]
+    arrived = lax.all_to_all(sending, "req", 0, 0, tiled=True)
     owner = jnp.where(came > 0, owner, 0).astype(jnp.int32)
 
     crossed = []
@@ -237,16 +238,18 @@
             jnp.bfloat16
         )
         crossed.append(across_rows(pair_sum))
-    barred = lax.optimization_barrier((tables, crossed[0][-1], crossed[-1][0]))
-    tables = barred[0]
-    chosen = tables[table_rows]
-    chosen_down = chosen[:, :, :cols]
-    up_parts = [chosen[:, :, cols:]]
+    early = lax.optimization_barrier((tables, crossed[0][0]))[0]
+    up_parts = [early[table_rows][:, :, cols:]]
     for k in range(1, mlp_count):
         pairs = [(m, (m + k) % mlp_count) for m in range(mlp_count)]
         up_parts.append(lax.ppermute(up_parts[0], "mlp", pairs))
     up_parts = jnp.stack(up_parts, axis=0)
     up_parts = up_parts[(mlp_index - jnp.arange(mlp_count, dtype=jnp.int32)) % mlp_count]
+    barred = lax.optimization_barrier(
+        (tables, crossed[0][-1], crossed[-1][0], up_parts, sending)
+    )
+    tables, up_parts = barred[0], barred[3]
+    chosen_down = tables[table_rows][:, :, :cols]
 
     every = jnp.concatenate([f[0].reshape(mlp_count, slot, local_heads * HD) for f in firsts])
     low_part = lax.dot_general(
@@ -260,6 +263,8 @@
 
     outs = []
     for c in range(own_requests):
+        if c > 0:
+            crossed[c][-1] = lax.optimization_barrier((crossed[c][-1], part))[0]
         mine = orders[c][:rows]
         low = low_all.reshape(rows, CORES, own_requests, low_all.shape[1], slot)[:, :, c]
         low = lax.dynamic_index_in_dim(low, core_index, axis=1, keepdims=False)

time: 228 us -> 210 us (0.921)
  waiting for transfers between devices: 56.3 us -> 39.2 us
    ppermute x3, waiting for transfers between devices: 27.9 us -> 2.06 us  [shards(): up_parts.append(lax.ppermute(up_parts[0], 'mlp', pairs))]
    all_gather x1, waiting for transfers between devices: 0.01 us -> 19.6 us  [shards(): tables = lax.all_gather(own_table, 'req', axis=0, tiled=True)]
    all_to_all x1, waiting for transfers between devices: 0.01 us -> 17.4 us  [shards(): arrived = lax.all_to_all(sending, 'req', 0, 0, tiled=True)]
    ppermute x2, waiting for transfers between devices: 17.4 us -> 0.01 us  [across_rows(): out.append(lax.ppermute(values, 'mlp', pairs))]
    ppermute x2, waiting for transfers between devices: 10.8 us -> 0.01 us  [shards(): feed = feed + lax.ppermute(send, 'mlp', pairs).astype(jnp.float32)]
    slice x1, local copies, waits for them, and re-layouts: 5 us -> 0.57 us  [shards(): own_tokens = tokens.reshape(rows, CORES, own_requests, slot, width)[:, :, c]]
    gather x2 -> x3, local copies, waits for them, and re-layouts: 4.13 us -> 8.33 us  [the longest x1 4.03 us: shards(): sending = fresh[leaving]]
    unnamed x77 -> x81, local copies, waits for them, and re-layouts: 8.51 us -> 11.5 us
  transfers between devices with their start and end apart: 18 -> 18, of which waited for: 5 -> 4; matrix products, arithmetic and copies ran while one was open for 40% -> 35% of each run, Pallas kernels for 11% -> 8%
where the time goes in v4:
time: 210 us
  matrix products  46 us (22%)
  waiting for transfers between devices  39.2 us (19%)
  local copies, waits for them, and re-layouts  36.9 us (18%)
  other arithmetic  28.8 us (14%)
  Pallas kernels  25.3 us (12%)
  starting transfers between devices  18.4 us (9%)
  between operations  14.9 us (7%)
    dot_general x2, matrix products, shards(): jnp.dot(expanded, down_weight, preferred_element_type=jnp.float32)  32.9 us
    all_gather x1, waiting for transfers between devices, shards(): tables = lax.all_gather(own_table, 'req', axis=0, tiled=True)  19.6 us
    pallas_call x2, Pallas kernels, attend(): pl.pallas_call(functools.partial(attend_body, local_heads, n_pages), grid...  18.6 us
    all_to_all x1, waiting for transfers between devices, shards(): arrived = lax.all_to_all(sending, 'req', 0, 0, tiled=True)  17.4 us
    unnamed x81, local copies, waits for them, and re-layouts  11.5 us
    dot_general x1, matrix products, shards(): jnp.dot(normed, joined_weight, preferred_element_type=jnp.float32)  10.6 us
    reduce_sum x3, other arithmetic, layer_norm(): mean = jnp.mean(values, axis=-1, keepdims=True)  7.88 us
    pallas_call x1, Pallas kernels, merge(): pl.pallas_call(lambda place, owner, came, *refs: merge_body(came, *refs),...  6.72 us
  transfers between devices with their start and end apart: 18, of which 4 were waited for; matrix products, arithmetic and copies ran while one was open for 35% of the time, Pallas kernels for 8%

profile of v4, /device:TPU:0, one launch (start us, length us, event | category | flops | bytes accessed | tf_op | source)
XLA Modules:
  0.0 209.5 jit_solution(11447447271132989909)
XLA Ops:
  8.2 1.6 pad_maximum_fusion.4
  9.9 3.0 %convert_reduce_fusion = f32[1024]{0:T(1024)S(1)} fusion(bf16[1024,2048]{1,0:T(8,128)(2,1)} %param.17), kind=kLoop, calls=%fused_computation.12 | loop fusion | flops 4193280 | bytes 4198400 | tf_op jit(solution)/shard_map/reduce_sum | solution.py:22
  15.2 10.6 %fusion.20.joined = bf16[1024,1536]{1,0:T(8,128)(2,1)S(1)} fusion(bf16[2048,1536]{1,0:T(8,128)(2,1)} %param.19, bf16[1024,2048]{1,0:T(8,128)(2,1)} %param.17, f32[2048]{0:T(1024)S(1)} %copy-done.37, f32[1024]{0:T(1024)S(1)} %add_rsqrt_fusion, f32[1024]{0:T(1024)S(1)} %broadcast_multiply_fusion), kind=kOutput, calls=%fused_computation.34 | convolution fusion | flops 6454509568 | bytes 13647872 | tf_op jit(solution)/shard_map/dot_general | solution.py:193
  25.9 9.3 %shard_map.176 = (bf16[512,512]{1,0:T(8,128)(2,1)S(1)}, bf16[4,128,1024]{2,1,0:T(8,128)(2,1)S(1)}, bf16[512,2048]{1,0:T(8,128)(2,1)S(1)}) custom-call(s32[4]{0:T(128)S(1)} %mul.163.order, s32[8,4]{1,0:T(8,128)S(1)} %gather_fusion, s32[8]{0:T(128)S(1)} %copy-done.15, f32[4]{0:T(128)S(1)} %multiply_exponential_fusion.slopes, ...), custom_call_target="tpu_custom_call" | custom-call | flops 3000000000 | bytes 10000000 | tf_op jit(solution)/shard_map/pallas_call | solution.py:88
  38.1 1.9 copy-done.4
  40.0 1.6 copy-done.6
  41.6 9.3 %shard_map.177 = (bf16[512,512]{1,0:T(8,128)(2,1)S(1)}, bf16[4,128,1024]{2,1,0:T(8,128)(2,1)S(1)}, bf16[512,2048]{1,0:T(8,128)(2,1)S(1)}) custom-call(s32[4]{0:T(128)S(1)} %get-tuple-element.45.order, s32[8,4]{1,0:T(8,128)S(1)} %gather_fusion, s32[8]{0:T(128)S(1)} %copy-done.15, f32[4]{0:T(128)S(1)} %multiply_exponential_fusion.slopes, ...), custom_call_target="tpu_custom_call" | custom-call | flops 3000000000 | bytes 10000000 | tf_op jit(solution)/shard_map/pallas_call | solution.py:88
  61.7 1.6 add_convert_fusion.3
  63.3 3.0 %collective-permute-start.1 = (bf16[256,2048]{1,0:T(8,128)(2,1)S(1)}, bf16[256,2048]{1,0:T(8,128)(2,1)}, u32[]{:S(2)}, u32[]{:S(2)}) collective-permute-start(bf16[256,2048]{1,0:T(8,128)(2,1)S(1)} %add_convert_fusion.3), channel_id=1, source_target_pairs={{0,2},{1,3},{2,0},{3,1},{4,6},{5,7},{6,4},{7,5},{8,10},{9,11},{10,... | collective-permute-start | bytes 3145736 | tf_op jit(solution)/shard_map/ppermute | solution.py:181
  66.4 4.0 %gather_fusion.5 = bf16[8,128,1024]{2,1,0:T(8,128)(2,1)} fusion(bf16[8,128,1024]{2,1,0:T(8,128)(2,1)} %constant_dynamic-update-slice_fusion.refs_0_, s32[1024]{0:T(1024)S(1)} %pad_clamp_fusion.4), kind=kCustom, calls=%fused_computation.5 | custom fusion | bytes 4194336 | tf_op jit(solution)/shard_map/gather | solution.py:229
  70.4 19.6 %all-gather.2.cloned.1.call-done = bf16[64,16,1024]{2,1,0:T(8,128)(2,1)} async-done(((bf16[8,16,1024]{2,1,0:T(8,128)(2,1)}), bf16[64,16,1024]{2,1,0:T(8,128)(2,1)}) %all-gather.2.cloned.1.call-update) | async-done | bytes 2097168 | tf_op jit(solution)/shard_map/all_gather | solution.py:190
  90.1 2.2 %gather_fusion.2 = bf16[8,16,1024]{2,1,0:T(8,128)(2,1)S(1)} fusion(bf16[64,16,1024]{2,1,0:T(8,128)(2,1)} %all-gather.2.cloned.1.call-done, s32[1024]{0:T(1024)S(1)} %pad_clamp_fusion.7), kind=kCustom, calls=%fused_computation.2 | custom fusion | bytes 524320 | tf_op jit(solution)/shard_map/gather | solution.py:242
  92.3 1.5 collective-permute-start.4
  93.9 1.4 collective-permute-start.5
  95.3 2.6 %add_convert_fusion.2 = bf16[256,2048]{1,0:T(8,128)(2,1)} fusion(bf16[256,2048]{1,0:T(8,128)(2,1)} %collective-permute-done.2, bf16[512,2048]{1,0:T(8,128)(2,1)S(1)} %copy-done.8), kind=kLoop, calls=%fused_computation.77 | loop fusion | flops 2097152 | bytes 3145728 | tf_op jit(solution)/shard_map/convert_element_type | solution.py:237
  100.6 2.2 %gather_fusion.6 = bf16[8,16,1024]{2,1,0:T(8,128)(2,1)S(1)} fusion(bf16[64,16,1024]{2,1,0:T(8,128)(2,1)} %all-gather.2.cloned.1.call-done, s32[1024]{0:T(1024)S(1)} %pad_clamp_fusion.7), kind=kCustom, calls=%fused_computation.6 | custom fusion | bytes 524320 | tf_op jit(solution)/shard_map/gather | solution.py:252
  105.2 1.5 collective-permute-start.7
  106.7 1.4 collective-permute-start.12
  112.0 2.1 %convert_reduce_fusion.2 = (f32[256]{0:T(256)S(1)}, bf16[256,2048]{1,0:T(8,128)(2,1)S(1)}) fusion(f32[2,128,2048]{2,1,0:T(8,128)S(1)} %pad_maximum_fusion, bf16[256,2048]{1,0:T(8,128)(2,1)} %collective-permute-done.1, bf16[256,2048]{1,0:T(8,128)(2,1)S(1)} %copy-done.25, bf16[2,1,1,128,2048]{4,3,2,1,0:T(8,128)(2,1)S(1)} %copy-done.29), kind=kLoop, calls=%fused_computation.40 | loop fusion | flops 4718336 | bytes 6292480 | tf_op jit(solution)/shard_map/reduce_sum | solution.py:22
  116.6 1.5 pad_maximum_fusion.1
  118.1 16.7 %convolution_convert_fusion.1 = bf16[512,2048]{1,0:T(8,128)(2,1)} fusion(bf16[2048,2048]{1,0:T(8,128)(2,1)} %param.27, bf16[2048,2048]{1,0:T(8,128)(2,1)} %param.26, bf16[256,2048]{1,0:T(8,128)(2,1)} %collective-permute-done.9, bf16[256,2048]{1,0:T(8,128)(2,1)} %copy-done.32), kind=kOutput, calls=%fused_computation.36 | convolution fusion | flops 8604614656 | bytes 20971520 | tf_op jit(solution)/shard_map/dot_general | solution.py:299
  134.8 2.8 %convert_reduce_fusion.1 = (f32[256]{0:T(256)S(1)}, bf16[256,2048]{1,0:T(8,128)(2,1)S(1)}) fusion(f32[2,128,2048]{2,1,0:T(8,128)} %pad_maximum_fusion.1, bf16[256,2048]{1,0:T(8,128)(2,1)} %collective-permute-done.12, bf16[256,2048]{1,0:T(8,128)(2,1)} %add_convert_fusion.2, bf16[2,1,1,128,2048]{4,3,2,1,0:T(8,128)(2,1)S(1)} %copy-done.28), kind=kLoop, calls=%fused_computation.38 | loop fusion | flops 4718336 | bytes 6292480 | tf_op jit(solution)/shard_map/reduce_sum | solution.py:22
  138.7 4.6 %all-to-all-start = ((bf16[8,128,1024]{2,1,0:T(8,128)(2,1)}), bf16[8,128,1024]{2,1,0:T(8,128)(2,1)}, u32[]{:S(2)}, u32[]{:S(2)}) async-start(bf16[8,128,1024]{2,1,0:T(8,128)(2,1)} %gather_fusion.5), calls=%async_computation | async-start | bytes 4194304 | tf_op jit(solution)/shard_map/all_to_all | solution.py:230
  144.8 2.3 %slice.135 = bf16[256,2048]{1,0:T(8,128)(2,1)} slice(bf16[512,2048]{1,0:T(8,128)(2,1)} %convolution_convert_fusion.1), slice={[256:512], [0:2048]} | slice | bytes 2097152 | tf_op jit(solution)/shard_map/slice | solution.py:302
  147.5 16.2 %convolution_convert_fusion = bf16[512,2048]{1,0:T(8,128)(2,1)} fusion(bf16[2048,2048]{1,0:T(8,128)(2,1)} %param.27, bf16[2048,2048]{1,0:T(8,128)(2,1)} %param.26, bf16[256,2048]{1,0:T(8,128)(2,1)} %collective-permute-done.13, bf16[256,2048]{1,0:T(8,128)(2,1)S(1)} %fusion.29), kind=kOutput, calls=%fused_computation.35 | convolution fusion | flops 8604614656 | bytes 20971520 | tf_op jit(solution)/shard_map/dot_general | solution.py:299
  163.7 1.4 slice.143
  166.6 1.8 add_convert_fusion.1
  169.3 1.3 collective-permute-start.11
  174.7 17.4 %all-to-all-done.refs_1_ = bf16[8,128,1024]{2,1,0:T(8,128)(2,1)} async-done(((bf16[8,128,1024]{2,1,0:T(8,128)(2,1)}), bf16[8,128,1024]{2,1,0:T(8,128)(2,1)}, u32[]{:S(2)}, u32[]{:S(2)}) %all-to-all-start) | async-done | bytes 2097184 | tf_op jit(solution)/shard_map/all_to_all | solution.py:230
  192.1 6.7 %shard_map.178 = bf16[8,128,1024]{2,1,0:T(8,128)(2,1)} custom-call(s32[8]{0:T(128)} %copy-done.20, s32[8]{0:T(128)} %compare_select_fusion.14.owner, s32[8]{0:T(128)} %convert_element_type.219.came, bf16[8,128,1024]{2,1,0:T(8,128)(2,1)} %constant_dynamic-update-slice_fusion.refs_0_, bf16[8,128,1024]{2,1,0:T(8,128)(2,1)} %all-to-all-done.refs_1_), custom_call_target="tpu_custom_call" | custom-call | tf_op jit(solution)/shard_map/pallas_call | solution.py:129
  198.8 1.4 fusion.63
  200.2 1.4 fusion.60
  (190 shorter events, 38.6 us)
Async XLA Ops:
  7.2 82.9 %all-gather.2.cloned.1.call-start = ((), (), s32[]{:S(2)}) async-start(), calls=%async_computation.1 | async-start | bytes 2359296 | tf_op jit(solution)/shard_map/all_gather | solution.py:190
  15.2 10.6 %copy-start.2 = (bf16[12,128,1024]{2,1,0:T(8,128)(2,1)S(1)}, bf16[12,128,1024]{2,1,0:T(8,128)(2,1)}, u32[]{:S(2)}) copy-start(bf16[12,128,1024]{2,1,0:T(8,128)(2,1)} %refs_3_.3) | copy-start | bytes 9437188
  15.2 10.6 %copy-start.5 = (bf16[512,2048]{1,0:T(8,128)(2,1)S(1)}, bf16[512,2048]{1,0:T(8,128)(2,1)}, u32[]{:S(2)}) copy-start(bf16[512,2048]{1,0:T(8,128)(2,1)} %refs_4_.3) | copy-start | bytes 6291460
  15.2 10.6 %copy-start.15 = (s32[8]{0:T(128)S(1)}, s32[8]{0:T(128)}, u32[]{:S(2)}) copy-start(s32[8]{0:T(128)} %lens.3) | copy-start | bytes 100
  25.8 9.4 %copy-start.3 = (bf16[1024,1536]{1,0:T(8,128)(2,1)}, bf16[1024,1536]{1,0:T(8,128)(2,1)S(1)}, u32[]{:S(2)}) copy-start(bf16[1024,1536]{1,0:T(8,128)(2,1)S(1)} %fusion.20.joined) | copy-start | bytes 9437188
  37.6 24.0 %collective-permute-start = (bf16[256,2048]{1,0:T(8,128)(2,1)}, bf16[256,2048]{1,0:T(8,128)(2,1)}, u32[]{:S(2)}, u32[]{:S(2)}) collective-permute-start(bf16[256,2048]{1,0:T(8,128)(2,1)} %slice.80), channel_id=1, source_target_pairs={{0,1},{1,0},{2,3},{3,2},{4,5},{5,4},{6,7},{7,6},{8,9},{9,8},{10,11... | collective-permute-start | bytes 3145736 | tf_op jit(solution)/shard_map/ppermute | solution.py:236
  51.0 4.1 %copy-start.35 = (s32[64]{0:T(128)S(1)}, s32[64]{0:T(128)}, u32[]{:S(2)}) copy-start(s32[64]{0:T(128)} %param.23) | copy-start | bytes 772
  51.0 4.2 %copy-start.21 = (s32[64]{0:T(128)S(1)}, s32[64]{0:T(128)}, u32[]{:S(2)}) copy-start(s32[64]{0:T(128)} %param.24) | copy-start | bytes 772
  51.0 4.9 %copy-start.12 = (bf16[4,128,1024]{2,1,0:T(8,128)(2,1)S(1)}, bf16[4,128,1024]{2,1,0:T(8,128)(2,1)}, u32[]{:S(2)}) copy-start(bf16[4,128,1024]{2,1,0:T(8,128)(2,1)} %copy-done.11) | copy-start | bytes 3145732
  53.3 42.0 %collective-permute-start.2 = (bf16[256,2048]{1,0:T(8,128)(2,1)}, bf16[256,2048]{1,0:T(8,128)(2,1)}, u32[]{:S(2)}, u32[]{:S(2)}) collective-permute-start(bf16[256,2048]{1,0:T(8,128)(2,1)} %slice.82), channel_id=1, source_target_pairs={{0,1},{1,0},{2,3},{3,2},{4,5},{5,4},{6,7},{7,6},{8,9},{9,8},{10,11... | collective-permute-start | bytes 3145736 | tf_op jit(solution)/shard_map/ppermute | solution.py:236
  54.4 3.8 %copy-start.20 = (s32[8]{0:T(128)}, s32[8]{0:T(128)S(1)}, u32[]{:S(2)}) copy-start(s32[8]{0:T(128)S(1)} %get-tuple-element.23.place) | copy-start | bytes 100
  63.3 7.1 %copy-start.24 = (bf16[256,2048]{1,0:T(8,128)(2,1)}, bf16[256,2048]{1,0:T(8,128)(2,1)S(1)}, u32[]{:S(2)}) copy-start(bf16[256,2048]{1,0:T(8,128)(2,1)S(1)} %add_convert_fusion.3) | copy-start | bytes 3145732
  63.3 37.2 %collective-permute-start.1 = (bf16[256,2048]{1,0:T(8,128)(2,1)S(1)}, bf16[256,2048]{1,0:T(8,128)(2,1)}, u32[]{:S(2)}, u32[]{:S(2)}) collective-permute-start(bf16[256,2048]{1,0:T(8,128)(2,1)S(1)} %add_convert_fusion.3), channel_id=1, source_target_pairs={{0,2},{1,3},{2,0},{3,1},{4,6},{5,7},{6,4},{7,5},{8,10},{9,11},{10,... | collective-permute-start | bytes 3145736 | tf_op jit(solution)/shard_map/ppermute | solution.py:181
  66.4 28.9 %copy-start.8 = (bf16[512,2048]{1,0:T(8,128)(2,1)S(1)}, bf16[512,2048]{1,0:T(8,128)(2,1)}, u32[]{:S(2)}) copy-start(bf16[512,2048]{1,0:T(8,128)(2,1)} %copy-done.7) | copy-start | bytes 6291460
  92.3 5.6 %collective-permute-start.3 = (bf16[8,16,512]{2,1,0:T(8,128)(2,1)S(1)}, bf16[8,16,512]{2,1,0:T(8,128)(2,1)S(1)}, u32[]{:S(2)}, u32[]{:S(2)}) collective-permute-start(bf16[8,16,512]{2,1,0:T(8,128)(2,1)S(1)} %get-tuple-element.37), channel_id=1, source_target_pairs={{0,1},{1,2},{2,3},{3,0},{4,5},{5,6},{6,7},{7,4},{8,9},{9,10},{10,1... | collective-permute-start | bytes 393224 | tf_op jit(solution)/shard_map/ppermute | solution.py:245
  92.3 6.4 %collective-permute-start.4 = (bf16[8,16,512]{2,1,0:T(8,128)(2,1)S(1)}, bf16[8,16,512]{2,1,0:T(8,128)(2,1)S(1)}, u32[]{:S(2)}, u32[]{:S(2)}) collective-permute-start(bf16[8,16,512]{2,1,0:T(8,128)(2,1)S(1)} %get-tuple-element.37), channel_id=1, source_target_pairs={{0,2},{1,3},{2,0},{3,1},{4,6},{5,7},{6,4},{7,5},{8,10},{9,11},{10,... | collective-permute-start | bytes 393224 | tf_op jit(solution)/shard_map/ppermute | solution.py:245
  93.9 6.0 %collective-permute-start.5 = (bf16[8,16,512]{2,1,0:T(8,128)(2,1)S(1)}, bf16[8,16,512]{2,1,0:T(8,128)(2,1)S(1)}, u32[]{:S(2)}, u32[]{:S(2)}) collective-permute-start(bf16[8,16,512]{2,1,0:T(8,128)(2,1)S(1)} %get-tuple-element.37), channel_id=1, source_target_pairs={{0,3},{1,0},{2,1},{3,2},{4,7},{5,4},{6,5},{7,6},{8,11},{9,8},{10,9... | collective-permute-start | bytes 393224 | tf_op jit(solution)/shard_map/ppermute | solution.py:245
  97.8 5.5 %copy-start.17 = (bf16[512,512]{1,0:T(8,128)(2,1)S(1)}, bf16[512,512]{1,0:T(8,128)(2,1)}, u32[]{:S(2)}) copy-start(bf16[512,512]{1,0:T(8,128)(2,1)} %copy-done.16) | copy-start | bytes 1572868
  97.8 5.5 %copy-start.19 = (bf16[512,512]{1,0:T(8,128)(2,1)S(1)}, bf16[512,512]{1,0:T(8,128)(2,1)}, u32[]{:S(2)}) copy-start(bf16[512,512]{1,0:T(8,128)(2,1)} %copy-done.18) | copy-start | bytes 1572868
  104.3 5.0 %collective-permute-start.6 = (bf16[8,16,128]{2,1,0:T(8,128)(2,1)S(1)}, bf16[8,16,128]{2,1,0:T(8,128)(2,1)S(1)}, u32[]{:S(2)}, u32[]{:S(2)}) collective-permute-start(bf16[8,16,128]{2,1,0:T(8,128)(2,1)S(1)} %gather_fusion.8), channel_id=1, source_target_pairs={{0,1},{1,2},{2,3},{3,0},{4,5},{5,6},{6,7},{7,4},{8,9},{9,10},{10,1... | collective-permute-start | bytes 98312 | tf_op jit(solution)/shard_map/ppermute | solution.py:261
  105.2 4.1 %collective-permute-start.7 = (bf16[8,16,128]{2,1,0:T(8,128)(2,1)S(1)}, bf16[8,16,128]{2,1,0:T(8,128)(2,1)S(1)}, u32[]{:S(2)}, u32[]{:S(2)}) collective-permute-start(bf16[8,16,128]{2,1,0:T(8,128)(2,1)S(1)} %gather_fusion.8), channel_id=1, source_target_pairs={{0,2},{1,3},{2,0},{3,1},{4,6},{5,7},{6,4},{7,5},{8,10},{9,11},{10,... | collective-permute-start | bytes 98312 | tf_op jit(solution)/shard_map/ppermute | solution.py:261
  106.7 2.6 %collective-permute-start.8 = (bf16[8,16,128]{2,1,0:T(8,128)(2,1)S(1)}, bf16[8,16,128]{2,1,0:T(8,128)(2,1)S(1)}, u32[]{:S(2)}, u32[]{:S(2)}) collective-permute-start(bf16[8,16,128]{2,1,0:T(8,128)(2,1)S(1)} %gather_fusion.8), channel_id=1, source_target_pairs={{0,3},{1,0},{2,1},{3,2},{4,7},{5,4},{6,5},{7,6},{8,11},{9,8},{10,9... | collective-permute-start | bytes 98312 | tf_op jit(solution)/shard_map/ppermute | solution.py:261
  106.7 28.1 %collective-permute-start.12 = (bf16[256,2048]{1,0:T(8,128)(2,1)}, bf16[256,2048]{1,0:T(8,128)(2,1)}, u32[]{:S(2)}, u32[]{:S(2)}) collective-permute-start(bf16[256,2048]{1,0:T(8,128)(2,1)} %add_convert_fusion.2), channel_id=1, source_target_pairs={{0,2},{1,3},{2,0},{3,1},{4,6},{5,7},{6,4},{7,5},{8,10},{9,11},{10,... | collective-permute-start | bytes 3145736 | tf_op jit(solution)/shard_map/ppermute | solution.py:181
  114.9 3.2 %collective-permute-start.9 = (bf16[256,2048]{1,0:T(8,128)(2,1)S(1)}, bf16[256,2048]{1,0:T(8,128)(2,1)}, u32[]{:S(2)}, u32[]{:S(2)}) collective-permute-start(bf16[256,2048]{1,0:T(8,128)(2,1)S(1)} %fusion.32), channel_id=1, source_target_pairs={{0,1},{1,0},{2,3},{3,2},{4,5},{5,4},{6,7},{7,6},{8,9},{9,8},{10,11... | collective-permute-start | bytes 3145736 | tf_op jit(solution)/shard_map/ppermute | solution.py:291
  118.1 16.7 %copy-start.28 = (bf16[2,1,1,128,2048]{4,3,2,1,0:T(8,128)(2,1)S(1)}, bf16[2,1,1,128,2048]{4,3,2,1,0:T(8,128)(2,1)}, u32[]{:S(2)}) copy-start(bf16[2,1,1,128,2048]{4,3,2,1,0:T(8,128)(2,1)} %constant_dynamic-slice_fusion) | copy-start | bytes 3145732
  138.5 9.0 %collective-permute-start.13 = (bf16[256,2048]{1,0:T(8,128)(2,1)S(1)}, bf16[256,2048]{1,0:T(8,128)(2,1)}, u32[]{:S(2)}, u32[]{:S(2)}) collective-permute-start(bf16[256,2048]{1,0:T(8,128)(2,1)S(1)} %fusion.29), channel_id=1, source_target_pairs={{0,1},{1,0},{2,3},{3,2},{4,5},{5,4},{6,7},{7,6},{8,9},{9,8},{10,11... | collective-permute-start | bytes 3145736 | tf_op jit(solution)/shard_map/ppermute | solution.py:291
  138.7 53.4 %all-to-all-start = ((bf16[8,128,1024]{2,1,0:T(8,128)(2,1)}), bf16[8,128,1024]{2,1,0:T(8,128)(2,1)}, u32[]{:S(2)}, u32[]{:S(2)}) async-start(bf16[8,128,1024]{2,1,0:T(8,128)(2,1)} %gather_fusion.5), calls=%async_computation | async-start | bytes 4194304 | tf_op jit(solution)/shard_map/all_to_all | solution.py:230
  147.1 19.5 %collective-permute-start.10 = (bf16[256,2048]{1,0:T(8,128)(2,1)}, bf16[256,2048]{1,0:T(8,128)(2,1)}, u32[]{:S(2)}, u32[]{:S(2)}) collective-permute-start(bf16[256,2048]{1,0:T(8,128)(2,1)} %slice.135), channel_id=1, source_target_pairs={{0,1},{1,0},{2,3},{3,2},{4,5},{5,4},{6,7},{7,6},{8,9},{9,8},{10,11... | collective-permute-start | bytes 3145736 | tf_op jit(solution)/shard_map/ppermute | solution.py:302
  165.1 5.5 %collective-permute-start.14 = (bf16[256,2048]{1,0:T(8,128)(2,1)S(1)}, bf16[256,2048]{1,0:T(8,128)(2,1)S(1)}, u32[]{:S(2)}, u32[]{:S(2)}) collective-permute-start(bf16[256,2048]{1,0:T(8,128)(2,1)S(1)} %slice.143), channel_id=1, source_target_pairs={{0,1},{1,0},{2,3},{3,2},{4,5},{5,4},{6,7},{7,6},{8,9},{9,8},{10,11... | collective-permute-start | bytes 3145736 | tf_op jit(solution)/shard_map/ppermute | solution.py:302
  166.6 4.0 %copy-start.31 = (bf16[512,2048]{1,0:T(8,128)(2,1)S(1)}, bf16[512,2048]{1,0:T(8,128)(2,1)}, u32[]{:S(2)}) copy-start(bf16[512,2048]{1,0:T(8,128)(2,1)} %convolution_convert_fusion) | copy-start | bytes 6291460
  169.3 29.5 %collective-permute-start.11 = (bf16[128,2048]{1,0:T(8,128)(2,1)}, bf16[128,2048]{1,0:T(8,128)(2,1)}, u32[]{:S(2)}, u32[]{:S(2)}) collective-permute-start(bf16[128,2048]{1,0:T(8,128)(2,1)} %dynamic-slice_bitcast_fusion.1), channel_id=1, source_target_pairs={{0,2},{1,3},{2,0},{3,1},{4,6},{5,7},{6,4},{7,5},{8,10},{9,11},{10,... | collective-permute-start | bytes 1572872 | tf_op jit(solution)/shard_map/ppermute | solution.py:314
  172.9 27.4 %collective-permute-start.15 = (bf16[128,2048]{1,0:T(8,128)(2,1)}, bf16[128,2048]{1,0:T(8,128)(2,1)}, u32[]{:S(2)}, u32[]{:S(2)}) collective-permute-start(bf16[128,2048]{1,0:T(8,128)(2,1)} %dynamic-slice_bitcast_fusion), channel_id=1, source_target_pairs={{0,2},{1,3},{2,0},{3,1},{4,6},{5,7},{6,4},{7,5},{8,10},{9,11},{10,... | collective-permute-start | bytes 1572872 | tf_op jit(solution)/shard_map/ppermute | solution.py:314
  (26 other events, 54.9 us)
Sparse Core Ops, SparseCore 0:
  38.2 51.8 all-gather.1
